TPU v7x, 1024 devices: a whole 4x8x16 slice. The times are simulated.
1024 devices in a mesh: gx: 16 (over z), gy: 64 (over y, x, core).
Axes of the slice: x: 4, y: 8, z: 16, core: 2. Of those that a mesh axis runs over, the one named last changes fastest.
Arguments:
- pdf: float32 [19, 256, 8192], P(None, 'gx', 'gy'), as said below
- grains: float32 [26, 16, 16384], P(None, 'gx', 'gy'), as said below
- grain_moves: int32 [16, 16384], P('gx', 'gy'), may hold values from 0 to 8, as said below
- owner_map: int32 [32, 128], P('gx', 'gy'), may hold values from 0 to 15, as said below
- link_lists: int32 [3, 32, 32768], P(None, 'gx', 'gy'), may hold values from 0 to 511, as said below
Outputs:
- moved_blocks: float32 [256, 64, 19, 512], P('gx', 'gy')
- new_grains: float32 [26, 16, 20480], P(None, 'gx', 'gy')
Inputs may be any that keep to these rules, and one draw needn't show every extreme that they name: `pdf`: each entry lies between 0.4 and 1.6 times its direction's lattice weight. `grains`: A grain's position lies inside the cells of the group that it belongs to after the move. `grain_moves`: at most 8 grains of one group move to any one of its eight neighbouring groups; every group moves at least one grain each way, and some group receives exactly 8 grains from each of its eight neighbours. `owner_map`: owners are gx indices in the block's own row of gy. At most 1 block of one group go to one owner, and in every row of gy one owner receives exactly 1 block from every group of that row. `link_lists`: row 0: a cell number of the block; row 1: a direction 1 to 18; row 2: a grain slot below 320. No cell appears twice among one block's links.
All inputs are finite; a program needn't handle non-finite values.
Results may differ from a plain program's by a relative error of at most 0.0003.
Values sent between devices are 32-bit elements; how exact they have to be, the bound alone decides.
No kernel may reach another device: no remote copies, remote signals or barrier semaphores. Data moves between devices by JAX's collectives and lax.ppermute only.
A program may use at most 64 MiB of HBM per device.

v0:
```python
import jax
import jax.numpy as jnp
import numpy as np
from jax import lax
from jax.sharding import PartitionSpec as P

Q = 19
E = 8
Z = 8
BXD = 2
BYD = 2
GCAP = 8
CAPP = 1
LB = 256
CB = 512


lattice_vel = np.array(
    [
        [0, 0, 0],
        [1, 0, 0],
        [-1, 0, 0],
        [0, 1, 0],
        [0, -1, 0],
        [0, 0, 1],
        [0, 0, -1],
        [1, 1, 0],
        [-1, -1, 0],
        [1, -1, 0],
        [-1, 1, 0],
        [1, 0, 1],
        [-1, 0, -1],
        [1, 0, -1],
        [-1, 0, 1],
        [0, 1, 1],
        [0, -1, -1],
        [0, 1, -1],
        [0, -1, 1],
    ],
    dtype=np.int32,
)
lattice_wts = np.array([1.0 / 3.0] + [1.0 / 18.0] * 6 + [1.0 / 36.0] * 12, dtype=np.float32)
opposite_dir = np.array(
    [0, 2, 1, 4, 3, 6, 5, 8, 7, 10, 9, 12, 11, 14, 13, 16, 15, 18, 17], dtype=np.int32
)
velocity_cols = lattice_vel.astype(np.float32)
moment_rows = np.stack(
    [
        np.ones(19, np.float32),
        velocity_cols[:, 0],
        velocity_cols[:, 1],
        velocity_cols[:, 2],
        velocity_cols[:, 0] * velocity_cols[:, 0],
        velocity_cols[:, 1] * velocity_cols[:, 1],
        velocity_cols[:, 2] * velocity_cols[:, 2],
        velocity_cols[:, 0] * velocity_cols[:, 1],
        velocity_cols[:, 0] * velocity_cols[:, 2],
        velocity_cols[:, 1] * velocity_cols[:, 2],
    ]
).astype(np.float32)
dirs_every = np.arange(19, dtype=np.int32)
viscosity_zero = 0.1
viscosity_limit = 0.01
relax_zero = 0.8
carreau_time = 20.0
carreau_power = 0.5


def shifted(block, axis, distance):
    devices = range(lax.axis_size(axis))
    route = [((i - distance) % len(devices), i) for i in devices]
    return lax.ppermute(block, axis, route)


def with_halo(block, sides, width):
    for axis, dim in sides:
        count = lax.axis_size(axis)
        forward = [(i, i + 1) for i in range(count - 1)]
        forward.append((count - 1, 0))
        backward = [(target, source) for source, target in forward]
        low = lax.ppermute(
            lax.slice_in_dim(block, block.shape[dim] - width, None, axis=dim), axis, forward
        )
        high = lax.ppermute(lax.slice_in_dim(block, 0, width, axis=dim), axis, backward)
        block = jnp.concatenate([low, block, high], axis=dim)
    return block


def collide(populations):
    moments = jnp.dot(jnp.asarray(moment_rows), populations, precision=lax.Precision.HIGHEST)
    density = moments[0]
    velocity = moments[1:4] / density
    projected = jnp.dot(jnp.asarray(velocity_cols), velocity, precision=lax.Precision.HIGHEST)
    speed_sq = jnp.sum(velocity * velocity, axis=0)
    equilibrium = (
        jnp.asarray(lattice_wts)[:, None]
        * density
        * (1.0 + 3.0 * projected + 4.5 * projected * projected - 1.5 * speed_sq)
    )
    density_third = density / 3.0
    stress_xx = moments[4] - density_third - density * velocity[0] * velocity[0]
    stress_yy = moments[5] - density_third - density * velocity[1] * velocity[1]
    stress_zz = moments[6] - density_third - density * velocity[2] * velocity[2]
    stress_xy = moments[7] - density * velocity[0] * velocity[1]
    stress_xz = moments[8] - density * velocity[0] * velocity[2]
    stress_yz = moments[9] - density * velocity[1] * velocity[2]
    contracted = (
        stress_xx * stress_xx
        + stress_yy * stress_yy
        + stress_zz * stress_zz
        + 2.0 * (stress_xy * stress_xy + stress_xz * stress_xz + stress_yz * stress_yz)
    )
    shear_rate = 1.5 / (density * relax_zero) * jnp.sqrt(2.0 * contracted)
    viscosity = viscosity_limit + (viscosity_zero - viscosity_limit) * (
        1.0 + (carreau_time * shear_rate) ** 2
    ) ** (0.5 * (carreau_power - 1.0))
    relax_time = 3.0 * viscosity + 0.5
    return populations - (populations - equilibrium) / relax_time


def pack_grains(own_grains, move_code, slot_cap):
    moving = move_code != 4
    region = jnp.where(move_code > 4, move_code - 1, move_code)
    matches = (move_code[None, :] == jnp.arange(9, dtype=jnp.int32)[:, None]).astype(jnp.int32)
    rank_of = jnp.sum(
        matches * (jnp.cumsum(matches, axis=1, dtype=jnp.int32) - 1), axis=0, dtype=jnp.int32
    )
    target = region * slot_cap + rank_of
    placing = jnp.logical_and(
        target[:, None] == jnp.arange(8 * slot_cap, dtype=jnp.int32)[None, :], moving[:, None]
    ).astype(jnp.float32)
    packed = jnp.dot(own_grains, placing, precision=lax.Precision.HIGHEST)
    kept_grains = own_grains * (move_code == 4).astype(jnp.float32)[None, :]
    return (kept_grains, packed)


def link_correction(cell_ids, direction_ids, picked, block_x, block_y):
    vel_table = jnp.asarray(velocity_cols)
    step_x = vel_table[:, 0][direction_ids]
    step_y = vel_table[:, 1][direction_ids]
    step_z = vel_table[:, 2][direction_ids]
    local_x = cell_ids // (E * Z)
    local_y = cell_ids // Z % E
    local_z = cell_ids % Z
    middle_x = (block_x * E + local_x).astype(jnp.float32) + 0.5 * step_x
    middle_y = (block_y * E + local_y).astype(jnp.float32) + 0.5 * step_y
    middle_z = local_z.astype(jnp.float32) + 0.5 * step_z
    rel_x = middle_x - picked[0]
    rel_y = middle_y - picked[1]
    rel_z = middle_z - picked[2]
    wall_x = picked[3] + picked[7] * rel_z - picked[8] * rel_y
    wall_y = picked[4] + picked[8] * rel_x - picked[6] * rel_z
    wall_z = picked[5] + picked[6] * rel_y - picked[7] * rel_x
    return (
        6.0
        * jnp.asarray(lattice_wts)[direction_ids]
        * (step_x * wall_x + step_y * wall_y + step_z * wall_z)
    )


def block_ranks(owners):
    count_blocks = owners.shape[-1]
    matching = owners[..., :, None] == owners[..., None, :]
    earlier = jnp.arange(count_blocks)[None, :] < jnp.arange(count_blocks)[:, None]
    return jnp.sum(jnp.logical_and(matching, earlier).astype(jnp.int32), axis=-1, dtype=jnp.int32)


def extend(populations, picks):
    plus_x, minus_x, plus_y, minus_y = picks
    count_dirs = populations.shape[0]
    width_x = populations.shape[1]
    ghosts_x = []
    for offset, chosen, first_cell in ((1, plus_x, width_x - 1), (-1, minus_x, 0)):
        rim_cells = lax.slice_in_dim(populations, first_cell, first_cell + 1, axis=1)[chosen]
        arrived = shifted(rim_cells, "gx", offset)
        ghosts_x.append(
            jnp.zeros((count_dirs, 1, populations.shape[2]), populations.dtype)
            .at[chosen]
            .set(arrived)
        )
    widened = jnp.concatenate([ghosts_x[0], populations, ghosts_x[1]], axis=1)
    length_y = widened.shape[2]
    ghosts_y = []
    for offset, chosen, first_cell in ((1, plus_y, length_y - Z), (-1, minus_y, 0)):
        rim_cells = lax.slice_in_dim(widened, first_cell, first_cell + Z, axis=2)[chosen]
        arrived = shifted(rim_cells, "gy", offset)
        ghosts_y.append(
            jnp.zeros((count_dirs, widened.shape[1], Z), widened.dtype).at[chosen].set(arrived)
        )
    return jnp.concatenate([ghosts_y[0], widened, ghosts_y[1]], axis=2)


def stream_flat(collided):
    tile_cells = collided.shape[1]
    row_width = (E + 2) * Z
    depth_index = jnp.arange(tile_cells, dtype=jnp.int32) % Z
    outputs = []
    for direction in range(19):
        step_x = int(lattice_vel[direction, 0])
        step_y = int(lattice_vel[direction, 1])
        step_z = int(lattice_vel[direction, 2])
        offset = step_x * row_width + step_y * Z + step_z
        layer_cells = jnp.roll(collided[direction], offset)
        if step_z == 1:
            layer_cells = jnp.where(
                depth_index == 0, jnp.roll(collided[direction], offset - Z), layer_cells
            )
        elif step_z == -1:
            layer_cells = jnp.where(
                depth_index == Z - 1, jnp.roll(collided[direction], offset + Z), layer_cells
            )
        outputs.append(layer_cells)
    return jnp.stack(outputs)


def interior_of(flat_tile):
    return flat_tile.reshape(Q, E + 2, E + 2, Z)[:, 1 : E + 1, 1 : E + 1, :].reshape(Q * CB)


def finish_tile(tile_cells, extra_rows):
    filled = extra_rows[2, 0]
    populations = jnp.where(filled > 0.5, tile_cells, jnp.asarray(lattice_wts)[:, None])
    collided = collide(populations)
    passed = interior_of(stream_flat(collided))
    interior = interior_of(collided)
    codes_int = extra_rows[1].astype(jnp.int32)
    target = jnp.asarray(opposite_dir)[codes_int // CB] * CB + codes_int % CB
    values = interior[codes_int] - extra_rows[0]
    return (passed.at[target].set(values) * filled).reshape(Q, CB)


def settle_tiles(parts):
    tile_part, extra_part = parts
    senders = tile_part.shape[0]
    item_count = tile_part.shape[1]
    finished = jax.vmap(finish_tile)(
        tile_part.reshape((senders * item_count,) + tile_part.shape[2:]),
        extra_part.reshape((senders * item_count,) + extra_part.shape[2:]),
    )
    return finished.reshape(senders, item_count, Q, CB)


def body(pdf, grains, grain_moves, owner_map, link_lists):
    group_size = lax.axis_size("gx")
    place_x = lax.axis_index("gx")
    place_y = lax.axis_index("gy")
    own_grains = grains[:, 0, :]
    move_codes = grain_moves[0]
    kept_grains, packed = pack_grains(own_grains, move_codes, GCAP)
    holder = packed[:, None, None, :]
    beside_all = with_halo(holder, (("gx", 1), ("gy", 2)), 1)
    regions = []
    for move_code in (0, 1, 2, 3, 5, 6, 7, 8):
        step_x = move_code // 3 - 1
        step_y = move_code % 3 - 1
        region = move_code if move_code < 4 else move_code - 1
        regions.append(
            beside_all[:, 1 - step_x, 1 - step_y, :][:, region * GCAP : (region + 1) * GCAP]
        )
    incoming = jnp.concatenate(regions, axis=1)
    grain_table = jnp.concatenate([kept_grains, incoming], axis=1)
    link_rows = link_lists.reshape(3, BXD * BYD, LB)
    local_number = jnp.arange(BXD * BYD, dtype=jnp.int32)[:, None]
    block_x = place_x * BXD + local_number // BYD
    block_y = place_y * BYD + local_number % BYD
    cell_ids, direction_ids, grain_ids = (link_rows[0], link_rows[1], link_rows[2])
    picked = grain_table[:, grain_ids]
    correction = link_correction(cell_ids, direction_ids, picked, block_x, block_y)
    source = direction_ids * CB + cell_ids
    owners = owner_map.reshape(-1)
    slot_index = owners * CAPP + block_ranks(owners)
    extended = extend(pdf, (dirs_every, dirs_every, dirs_every, dirs_every))
    tile_list = []
    for tile_x in range(BXD):
        for tile_y in range(BYD):
            tile_list.append(
                extended[
                    :, tile_x * E : tile_x * E + E + 2, tile_y * E * Z : (tile_y * E + E + 2) * Z
                ].reshape(Q, -1)
            )
    tile_stack = jnp.stack(tile_list)
    extras = jnp.stack([correction, source.astype(jnp.float32), jnp.ones_like(correction)], axis=1)
    send_tiles = (
        jnp.zeros((group_size * CAPP,) + tile_stack.shape[1:], jnp.float32)
        .at[slot_index]
        .set(tile_stack)
    )
    send_extras = (
        jnp.zeros((group_size * CAPP,) + extras.shape[1:], jnp.float32).at[slot_index].set(extras)
    )
    send_tiles = send_tiles.reshape((group_size, CAPP) + tile_stack.shape[1:])
    send_extras = send_extras.reshape((group_size, CAPP) + extras.shape[1:])
    moved_blocks = settle_tiles(
        (
            lax.all_to_all(send_tiles, "gx", split_axis=0, concat_axis=0, tiled=True),
            lax.all_to_all(send_extras, "gx", split_axis=0, concat_axis=0, tiled=True),
        )
    )
    return (moved_blocks, grain_table[:, None, :])


def solution(mesh):
    in_specs = (
        P(None, "gx", "gy"),
        P(None, "gx", "gy"),
        P("gx", "gy"),
        P("gx", "gy"),
        P(None, "gx", "gy"),
    )
    out_specs = (P("gx", "gy", None, None), P(None, "gx", "gy"))
    return jax.shard_map(body, mesh=mesh, in_specs=in_specs, out_specs=out_specs, check_vma=False)
```

profile of v0, /device:TPU:71, one launch (start us, length us, event | category | flops | bytes accessed | tf_op | source)
XLA Modules:
  0.0 437.5 jit_solution(9275884077714305928)
XLA Ops:
  7.2 4.0 collective-permute-start
  13.5 4.0 collective-permute-start.4
  18.1 13.1 %collective-permute-start.5 = (f32[19,1,128]{2,0,1:T(8,128)S(1)}, f32[19,1,128]{2,0,1:T(8,128)S(1)}, u32[]{:S(2)}, u32[]{:S(2)}) collective-permute-start(f32[19,1,128]{2,0,1:T(8,128)S(1)} %bitcast.488), channel_id=1, source_target_pairs={{64,0},{128,64},{192,128},{256,192},{320,256},{384,320},{448,384},... | collective-permute-start | bytes 29192 | tf_op jit(solution)/shard_map/ppermute | solution.py:72
  33.7 6.6 %gather_fusion = f32[1024]{0:T(1024)S(1)} fusion(f32[19]{0:T(128)S(1)} %copy-done.1, s32[1024]{0:T(1024)S(1)} %broadcast_clamp_fusion.2), kind=kCustom, calls=%fused_computation | custom fusion | bytes 12288 | tf_op jit(solution)/shard_map/gather | solution.py:156
  40.4 4.2 collective-permute-start.3
  49.3 5.8 %collective-permute-start.6 = (f32[19,18,8]{2,1,0:T(8,128)S(1)}, f32[19,18,8]{2,1,0:T(8,128)S(1)}, u32[]{:S(2)}, u32[]{:S(2)}) collective-permute-start(f32[19,18,8]{2,1,0:T(8,128)S(1)} %gather_fusion.7), channel_id=1, source_target_pairs={{63,0},{0,1},{1,2},{2,3},{3,4},{4,5},{5,6},{6,7},{7,8},{8,9},{9,10... | collective-permute-start | bytes 32840 | tf_op jit(solution)/shard_map/ppermute | solution.py:72
  55.1 6.6 %gather_fusion.4 = f32[1024]{0:T(1024)S(1)} fusion(f32[19]{0:T(128)S(1)} %copy-done.4, s32[1024]{0:T(1024)S(1)} %broadcast_clamp_fusion.2), kind=kCustom, calls=%fused_computation.4 | custom fusion | bytes 12288 | tf_op jit(solution)/shard_map/gather | solution.py:140
  61.7 6.6 %gather_fusion.3 = f32[1024]{0:T(1024)S(1)} fusion(f32[19]{0:T(128)S(1)} %copy-done.3, s32[1024]{0:T(1024)S(1)} %broadcast_clamp_fusion.2), kind=kCustom, calls=%fused_computation.3 | custom fusion | bytes 12288 | tf_op jit(solution)/shard_map/gather | solution.py:141
  68.3 6.6 %gather_fusion.1 = f32[1024]{0:T(1024)S(1)} fusion(f32[19]{0:T(128)S(1)} %copy-done.2, s32[1024]{0:T(1024)S(1)} %broadcast_clamp_fusion.2), kind=kCustom, calls=%fused_computation.1 | custom fusion | bytes 12288 | tf_op jit(solution)/shard_map/gather | solution.py:139
  82.9 2.8 gather_fusion.2
  87.4 7.1 %all-to-all-start = ((f32[16,1,3,256]{3,1,2,0:T(1,128)}), f32[16,1,3,256]{3,1,2,0:T(1,128)S(1)}, u32[]{:S(2)}, u32[]{:S(2)}) async-start(f32[16,1,3,256]{3,1,2,0:T(1,128)} %copy.391), calls=%async_computation | async-start | bytes 98304 | tf_op jit(solution)/shard_map/all_to_all | solution.py:296
  98.3 7.0 %all-to-all-done = f32[16,1,3,256]{3,1,2,0:T(1,128)S(1)} async-done(((f32[16,1,3,256]{3,1,2,0:T(1,128)}), f32[16,1,3,256]{3,1,2,0:T(1,128)S(1)}, u32[]{:S(2)}, u32[]{:S(2)}) %all-to-all-start) | async-done | bytes 49184 | tf_op jit(solution)/shard_map/all_to_all | solution.py:296
  105.4 4.6 %all-to-all-start.1 = ((f32[16,1,19,800]{3,1,2,0:T(1,128)}), f32[16,1,19,800]{3,1,2,0:T(1,128)S(1)}, u32[]{:S(2)}, u32[]{:S(2)}) async-start(f32[16,1,19,800]{3,1,2,0:T(1,128)} %copy.402), calls=%async_computation.1 | async-start | bytes 2179072 | tf_op jit(solution)/shard_map/all_to_all | solution.py:295
  111.3 24.7 %gather_fusion.9 = s32[4096]{0:T(1024)S(1)} fusion(s32[19]{0:T(128)S(1)} %copy-done, s32[4096]{0:T(1024)S(1)} %broadcast_clamp_fusion), kind=kCustom, calls=%fused_computation.9 | custom fusion | bytes 49152 | tf_op jit(solution)/shard_map/vmap()/gather | solution.py:227
  137.5 23.6 %all-to-all-done.1 = f32[16,1,19,800]{3,1,2,0:T(1,128)S(1)} async-done(((f32[16,1,19,800]{3,1,2,0:T(1,128)}), f32[16,1,19,800]{3,1,2,0:T(1,128)S(1)}, u32[]{:S(2)}, u32[]{:S(2)}) %all-to-all-start.1) | async-done | bytes 972832 | tf_op jit(solution)/shard_map/all_to_all | solution.py:295
  186.1 4.6 %copy.420 = f32[16,19,800]{1,2,0:T(8,128)} copy(f32[16,19,800]{2,0,1:T(8,128)S(1)} %fusion.7) | data formatting | bytes 1945600 | tf_op jit(solution)/shard_map/vmap()/sub | solution.py:118
  197.6 4.6 %copy.418 = f32[16,19,800]{1,2,0:T(8,128)} copy(f32[16,19,800]{2,0,1:T(8,128)S(1)} %bitcast.460) | data formatting | bytes 1945600 | tf_op jit(solution)/shard_map/vmap()/transpose | solution.py:217
  202.2 4.7 %slice.732 = f32[16,19,8,8,8]{1,4,3,2,0:T(8,128)} slice(f32[16,19,10,10,8]{1,4,3,2,0:T(8,128)} %bitcast.458), slice={[0:16], [0:19], [1:9], [1:9], [0:8]} | slice | bytes 1245184 | tf_op jit(solution)/shard_map/vmap()/slice | solution.py:217
  206.9 4.9 %slice.734 = f32[16,19,8,8,8]{1,4,3,2,0:T(8,128)} slice(f32[16,19,10,10,8]{1,4,3,2,0:T(8,128)} %bitcast.457), slice={[0:16], [0:19], [1:9], [1:9], [0:8]} | slice | bytes 1245184 | tf_op jit(solution)/shard_map/vmap()/slice | solution.py:217
  211.7 8.0 %copy.421 = f32[16,19,8,8,8]{0,4,3,2,1:T(8,128)} copy(f32[16,19,8,8,8]{1,4,3,2,0:T(8,128)} %slice.734) | data formatting | bytes 1245184 | tf_op jit(solution)/shard_map/vmap()/slice | solution.py:217
  219.7 180.6 %gather_fusion.10 = f32[4096]{0:T(1024)S(1)} fusion(f32[16,9728]{0,1:T(8,128)} %bitcast.456, s32[4096]{0:T(1024)S(1)} %bitcast.455), kind=kCustom, calls=%fused_computation.10 | custom fusion | bytes 65536 | tf_op jit(solution)/shard_map/vmap()/gather | solution.py:228
  400.3 11.6 %copy.419 = f32[16,19,8,8,8]{4,3,2,1,0:T(8,128)} copy(f32[16,19,8,8,8]{1,4,3,2,0:T(8,128)} %slice.732) | data formatting | bytes 1245184 | tf_op jit(solution)/shard_map/vmap()/slice | solution.py:217
  411.9 7.5 %reshape.1599 = f32[155648]{0:T(1024)S(1)} reshape(f32[16,19,8,8,8]{4,3,2,1,0:T(8,128)} %copy.419) | data formatting | bytes 1245184
  419.4 15.8 %scatter_fusion.4 = f32[155648]{0:T(1024)S(1)} fusion(f32[155648]{0:T(1024)S(1)} %reshape.1599, s32[4096]{0:T(1024)S(1)} %bitcast.474, f32[4096]{0:T(1024)S(1)} %bitcast.475), kind=kCustom, calls=%fused_computation.17 | custom fusion | bytes 65536
  (280 shorter events, 66.3 us)
Async XLA Ops:
  0.6 33.1 %copy-start.1 = (f32[19]{0:T(128)S(1)}, f32[19]{0:T(128)}, u32[]{:S(2)}) copy-start(f32[19]{0:T(128)} %constant.193.clone) | copy-start | bytes 232
  5.3 35.1 %collective-permute-start.1 = (f32[26,1,1,64]{3,0,2,1:T(8,128)S(1)}, f32[26,1,1,64]{3,0,2,1:T(8,128)S(1)}, u32[]{:S(2)}, u32[]{:S(2)}) collective-permute-start(f32[26,1,1,64]{3,0,2,1:T(8,128)S(1)} %convolution_bitcast_fusion), channel_id=1, source_target_pairs={{64,0},{128,64},{192,128},{256,192},{320,256},{384,320},{448,384},... | collective-permute-start | bytes 19976 | tf_op jit(solution)/shard_map/ppermute | solution.py:84
  7.2 33.2 %collective-permute-start = (f32[26,1,1,64]{3,0,2,1:T(8,128)S(1)}, f32[26,1,1,64]{3,0,2,1:T(8,128)S(1)}, u32[]{:S(2)}, u32[]{:S(2)}) collective-permute-start(f32[26,1,1,64]{3,0,2,1:T(8,128)S(1)} %convolution_bitcast_fusion), channel_id=1, source_target_pairs={{0,64},{64,128},{128,192},{192,256},{256,320},{320,384},{384,448},... | collective-permute-start | bytes 19976 | tf_op jit(solution)/shard_map/ppermute | solution.py:81
  13.5 31.2 %collective-permute-start.4 = (f32[19,1,128]{2,0,1:T(8,128)S(1)}, f32[19,1,128]{2,0,1:T(8,128)S(1)}, u32[]{:S(2)}, u32[]{:S(2)}) collective-permute-start(f32[19,1,128]{2,0,1:T(8,128)S(1)} %bitcast.489), channel_id=1, source_target_pairs={{960,0},{0,64},{64,128},{128,192},{192,256},{256,320},{320,384},{3... | collective-permute-start | bytes 29192 | tf_op jit(solution)/shard_map/ppermute | solution.py:72
  18.1 27.3 %collective-permute-start.5 = (f32[19,1,128]{2,0,1:T(8,128)S(1)}, f32[19,1,128]{2,0,1:T(8,128)S(1)}, u32[]{:S(2)}, u32[]{:S(2)}) collective-permute-start(f32[19,1,128]{2,0,1:T(8,128)S(1)} %bitcast.488), channel_id=1, source_target_pairs={{64,0},{128,64},{192,128},{256,192},{320,256},{384,320},{448,384},... | collective-permute-start | bytes 29192 | tf_op jit(solution)/shard_map/ppermute | solution.py:72
  33.7 6.6 %copy-start.28 = (f32[26,1,256]{2,1,0:T(1,128)S(1)}, f32[26,1,256]{2,1,0:T(1,128)}, u32[]{:S(2)}) copy-start(f32[26,1,256]{2,1,0:T(1,128)} %param.19) | copy-start | bytes 79876
  33.7 12.3 %copy-start.5 = (f32[19,16,128]{2,1,0:T(8,128)S(1)}, f32[19,16,128]{2,1,0:T(8,128)}, u32[]{:S(2)}) copy-start(f32[19,16,128]{2,1,0:T(8,128)} %param.18) | copy-start | bytes 466948
  40.4 40.5 %collective-permute-start.3 = (f32[26,3,1,64]{3,0,2,1:T(8,128)S(1)}, f32[26,3,1,64]{3,0,2,1:T(8,128)S(1)}, u32[]{:S(2)}, u32[]{:S(2)}) collective-permute-start(f32[26,3,1,64]{3,0,2,1:T(8,128)S(1)} %pad_maximum_fusion.10), channel_id=1, source_target_pairs={{0,1},{1,2},{2,3},{3,4},{4,5},{5,6},{6,7},{7,8},{8,9},{9,10},{10,1... | collective-permute-start | bytes 59912 | tf_op jit(solution)/shard_map/ppermute | solution.py:81
  46.0 9.0 %copy-start.4 = (f32[19]{0:T(128)S(1)}, f32[19]{0:T(128)}, u32[]{:S(2)}) copy-start(f32[19]{0:T(128)} %constant.213) | copy-start | bytes 232
  47.4 29.7 %collective-permute-start.7 = (f32[19,18,8]{2,1,0:T(8,128)S(1)}, f32[19,18,8]{2,1,0:T(8,128)S(1)}, u32[]{:S(2)}, u32[]{:S(2)}) collective-permute-start(f32[19,18,8]{2,1,0:T(8,128)S(1)} %gather_fusion.8), channel_id=1, source_target_pairs={{1,0},{2,1},{3,2},{4,3},{5,4},{6,5},{7,6},{8,7},{9,8},{10,9},{11,1... | collective-permute-start | bytes 32840 | tf_op jit(solution)/shard_map/ppermute | solution.py:72
  49.3 29.7 %collective-permute-start.6 = (f32[19,18,8]{2,1,0:T(8,128)S(1)}, f32[19,18,8]{2,1,0:T(8,128)S(1)}, u32[]{:S(2)}, u32[]{:S(2)}) collective-permute-start(f32[19,18,8]{2,1,0:T(8,128)S(1)} %gather_fusion.7), channel_id=1, source_target_pairs={{63,0},{0,1},{1,2},{2,3},{3,4},{4,5},{5,6},{6,7},{7,8},{8,9},{9,10... | collective-permute-start | bytes 32840 | tf_op jit(solution)/shard_map/ppermute | solution.py:72
  55.1 6.6 %copy-start.3 = (f32[19]{0:T(128)S(1)}, f32[19]{0:T(128)}, u32[]{:S(2)}) copy-start(f32[19]{0:T(128)} %constant.211) | copy-start | bytes 232
  61.7 6.6 %copy-start.2 = (f32[19]{0:T(128)S(1)}, f32[19]{0:T(128)}, u32[]{:S(2)}) copy-start(f32[19]{0:T(128)} %constant.209) | copy-start | bytes 232
  75.0 7.5 %collective-permute-start.2 = (f32[26,3,1,64]{3,0,2,1:T(8,128)S(1)}, f32[26,3,1,64]{3,0,2,1:T(8,128)S(1)}, u32[]{:S(2)}, u32[]{:S(2)}) collective-permute-start(f32[26,3,1,64]{3,0,2,1:T(8,128)S(1)} %pad_maximum_fusion.10), channel_id=1, source_target_pairs={{1,0},{2,1},{3,2},{4,3},{5,4},{6,5},{7,6},{8,7},{9,8},{10,9},{11,1... | collective-permute-start | bytes 59912 | tf_op jit(solution)/shard_map/ppermute | solution.py:84
  87.4 17.9 %all-to-all-start = ((f32[16,1,3,256]{3,1,2,0:T(1,128)}), f32[16,1,3,256]{3,1,2,0:T(1,128)S(1)}, u32[]{:S(2)}, u32[]{:S(2)}) async-start(f32[16,1,3,256]{3,1,2,0:T(1,128)} %copy.391), calls=%async_computation | async-start | bytes 98304 | tf_op jit(solution)/shard_map/all_to_all | solution.py:296
  98.3 12.9 %copy-start = (s32[19]{0:T(128)S(1)}, s32[19]{0:T(128)}, u32[]{:S(2)}) copy-start(s32[19]{0:T(128)} %constant.196.clone) | copy-start | bytes 232
  105.4 55.7 %all-to-all-start.1 = ((f32[16,1,19,800]{3,1,2,0:T(1,128)}), f32[16,1,19,800]{3,1,2,0:T(1,128)S(1)}, u32[]{:S(2)}, u32[]{:S(2)}) async-start(f32[16,1,19,800]{3,1,2,0:T(1,128)} %copy.402), calls=%async_computation.1 | async-start | bytes 2179072 | tf_op jit(solution)/shard_map/all_to_all | solution.py:295
  111.3 24.8 %copy-start.35 = (s32[2]{0:T(128)S(1)}, s32[2]{0:T(128)}, u32[]{:S(2)}) copy-start(s32[2]{0:T(128)} %constant.201) | copy-start | bytes 28
  111.3 24.9 %copy-start.34 = (s32[2]{0:T(128)S(1)}, s32[2]{0:T(128)}, u32[]{:S(2)}) copy-start(s32[2]{0:T(128)} %constant.204) | copy-start | bytes 28
  137.5 23.7 %copy-start.30 = (f32[10,19,1]{1,0,2:T(8,128)S(1)}, f32[10,19,1]{1,0,2:T(8,128)}, u32[]{:S(2)}) copy-start(f32[10,19,1]{1,0,2:T(8,128)} %constant.228) | copy-start | bytes 2284
  186.0 8.1 %copy-start.29 = (pred[800]{0:T(1024)(128)(4,1)S(1)}, pred[800]{0:T(1024)(128)(4,1)}, u32[]{:S(2)}) copy-start(pred[800]{0:T(1024)(128)(4,1)} %fusion.100) | copy-start | bytes 2404
  190.8 6.4 %copy-start.16 = (f32[1,16,9]{2,1,0:T(8,128)S(1)}, f32[1,16,9]{2,1,0:T(8,128)}, u32[]{:S(2)}) copy-start(f32[1,16,9]{2,1,0:T(8,128)} %slice_bitcast_fusion.56) | copy-start | bytes 1732
  190.9 6.4 %copy-start.17 = (f32[1,16,1]{2,1,0:T(8,128)S(1)}, f32[1,16,1]{2,1,0:T(8,128)}, u32[]{:S(2)}) copy-start(f32[1,16,1]{2,1,0:T(8,128)} %slice_bitcast_fusion.57) | copy-start | bytes 196
  411.9 7.5 %copy-start.10 = (s32[2,2,8,128]{3,1,2,0:T(2,128)S(1)}, s32[2,2,8,128]{3,1,2,0:T(2,128)}, u32[]{:S(2)}) copy-start(s32[2,2,8,128]{3,1,2,0:T(2,128)} %copy.437) | copy-start | bytes 49156
  (22 other events, 114.9 us)
where the time goes:
time: 442 us; the launch traced here: 437 us
  local copies, waits for them, and re-layouts  336 us (76%)
  starting transfers between devices  48.6 us (11%)
  waiting for transfers between devices  31.9 us (7%)
  other arithmetic  15.2 us (3%)
    gather x2, local copies, waits for them, and re-layouts, finish_tile(): values = interior[codes_int] - extra_rows[0]  181 us
    slice x4, local copies, waits for them, and re-layouts, interior_of(): flat_tile.reshape(Q, E + 2, E + 2, Z)[:, 1:E + 1, 1:E + 1, :]  29.1 us
    unnamed x85, local copies, waits for them, and re-layouts  25.8 us
    ppermute x4, starting transfers between devices, shifted(): return lax.ppermute(block, axis, route)  24.8 us
    gather x1, local copies, waits for them, and re-layouts, finish_tile(): target = jnp.asarray(opposite_dir)[codes_int // CB] * CB + codes_int % CB  24.7 us
    all_to_all x1, waiting for transfers between devices, body(): lax.all_to_all(send_tiles, 'gx', split_axis=0, concat_axis=0, tiled=True)  23.6 us
  transfers between devices with their start and end apart: 10, of which 3 were waited for; matrix products, arithmetic and copies ran while one was open for 16% of the time, Pallas kernels for 0%

commit v1 on v0

v1 whole, which is shorter than its diff:
```python
import jax
import jax.numpy as jnp
import numpy as np
from jax import lax
from jax.experimental import pallas as pl
from jax.experimental.pallas import tpu as pltpu
from jax.sharding import PartitionSpec as P

Q = 19
E = 8
Z = 8
ROWS = 16
LANE = 128
GV = 26

CX = (0, 1, -1, 0, 0, 0, 0, 1, -1, 1, -1, 1, -1, 1, -1, 0, 0, 0, 0)
CY = (0, 0, 0, 1, -1, 0, 0, 1, -1, -1, 1, 0, 0, 0, 0, 1, -1, 1, -1)
CZ = (0, 0, 0, 0, 0, 1, -1, 0, 0, 0, 0, 1, -1, -1, 1, 1, -1, -1, 1)
OPP = (0, 2, 1, 4, 3, 6, 5, 8, 7, 10, 9, 12, 11, 14, 13, 16, 15, 18, 17)
WTS = tuple(float(np.float32(w)) for w in [1.0 / 3.0] + [1.0 / 18.0] * 6 + [1.0 / 36.0] * 12)
W6_AXIS = float(np.float32(6.0) * np.float32(1.0 / 18.0))
W6_DIAG = float(np.float32(6.0) * np.float32(1.0 / 36.0))
XUP = tuple(q for q in range(Q) if CX[q] == 1)
XDN = tuple(q for q in range(Q) if CX[q] == -1)
YUP = tuple(q for q in range(Q) if CY[q] == 1)
YDN = tuple(q for q in range(Q) if CY[q] == -1)
CODES = (0, 1, 2, 3, 5, 6, 7, 8)

F32 = jnp.float32
BF16 = jnp.bfloat16
I32 = jnp.int32


def iota(shape, dim):
    return lax.broadcasted_iota(I32, shape, dim)


def split3(value):
    high = value.astype(BF16)
    rest = value - high.astype(F32)
    middle = rest.astype(BF16)
    low = (rest - middle.astype(F32)).astype(BF16)
    return high, middle, low


def dot_nt(a, b):
    return lax.dot_general(a, b, (((1,), (1,)), ((), ())), preferred_element_type=F32)


def dot_nn(a, b):
    return lax.dot_general(a, b, (((1,), (0,)), ((), ())), preferred_element_type=F32)


def one_of(index, chosen):
    hit = index == chosen[0]
    for value in chosen[1:]:
        hit = jnp.logical_or(hit, index == value)
    return hit


def z_shift(plane, step, lane):
    depth = lane % Z
    if step == 1:
        return jnp.where(depth == 0, pltpu.roll(plane, LANE - (Z - 1), 1), pltpu.roll(plane, 1, 1))
    if step == -1:
        return jnp.where(depth == Z - 1, pltpu.roll(plane, Z - 1, 1), pltpu.roll(plane, LANE - 1, 1))
    return plane


def collide(f):
    s = {q: f[q] + f[q + 1] for q in range(1, Q, 2)}
    d = {q: f[q] - f[q + 1] for q in range(1, Q, 2)}
    pxx = s[1] + s[7] + s[9] + s[11] + s[13]
    pyy = s[3] + s[7] + s[9] + s[15] + s[17]
    pzz = s[5] + s[11] + s[13] + s[15] + s[17]
    pxy = s[7] - s[9]
    pxz = s[11] - s[13]
    pyz = s[15] - s[17]
    rho = f[0] + s[1] + s[3] + s[5] + s[7] + s[9] + s[11] + s[13] + s[15] + s[17]
    inv_rho = 1.0 / rho
    ux = (d[1] + d[7] + d[9] + d[11] + d[13]) * inv_rho
    uy = (d[3] + d[7] - d[9] + d[15] + d[17]) * inv_rho
    uz = (d[5] + d[11] - d[13] + d[15] - d[17]) * inv_rho
    third = rho * (1.0 / 3.0)
    sxx = pxx - third - rho * ux * ux
    syy = pyy - third - rho * uy * uy
    szz = pzz - third - rho * uz * uz
    sxy = pxy - rho * ux * uy
    sxz = pxz - rho * ux * uz
    syz = pyz - rho * uy * uz
    contracted = sxx * sxx + syy * syy + szz * szz + 2.0 * (sxy * sxy + sxz * sxz + syz * syz)
    rate = 1.5 / 0.8 * inv_rho * jnp.sqrt(2.0 * contracted)
    scaled = 20.0 * rate
    viscosity = 0.01 + 0.09 * lax.rsqrt(jnp.sqrt(1.0 + scaled * scaled))
    omega = 1.0 / (3.0 * viscosity + 0.5)
    speed = 1.0 - 1.5 * (ux * ux + uy * uy + uz * uz)
    vel = (ux, uy, uz)
    out = [None] * Q
    out[0] = f[0] - (f[0] - WTS[0] * rho * speed) * omega
    for q in range(1, Q, 2):
        proj = None
        for comp, step in zip(vel, (CX[q], CY[q], CZ[q])):
            if step:
                term = comp if step > 0 else -comp
                proj = term if proj is None else proj + term
        scale = WTS[q] * rho
        even = scale * (speed + 4.5 * proj * proj)
        odd = scale * (3.0 * proj)
        out[q] = f[q] - (f[q] - (even + odd)) * omega
        out[q + 1] = f[q + 1] - (f[q + 1] - (even - odd)) * omega
    return out


def first_kernel(pdf_ref, grains_ref, moves_ref, col_ref, up_ref, dn_ref):
    lane = iota((ROWS, LANE), 1)
    col = collide([pdf_ref[q] for q in range(Q)])
    for q in range(Q):
        col_ref[q] = col[q]
    for ref, chosen, edge in ((up_ref, YUP, LANE - Z), (dn_ref, YDN, 0)):
        rim = jnp.zeros((ROWS, LANE), F32)
        for k, q in enumerate(chosen):
            moved = pltpu.roll(z_shift(col[q], CZ[q], lane), (k * Z - edge) % LANE, 1)
            rim = jnp.where(lane // Z == k, moved, rim)
        ref[0:ROWS, :] = rim
    moves = moves_ref[...]
    count = moves.shape[1]
    matches = (iota((16, count), 0) == moves).astype(F32)
    earlier = (iota((count, count), 0) < iota((count, count), 1)).astype(F32).astype(BF16)
    before = dot_nn(matches.astype(BF16), earlier)
    rank = jnp.sum(matches * before, axis=0, keepdims=True).astype(I32)
    region = jnp.where(moves > 4, moves - 1, moves)
    target = jnp.where(moves == 4, -1, region * 8 + rank)
    placing = (iota((LANE, count), 0) == target).astype(F32).astype(BF16)
    own = grains_ref[:, 0, :]
    high, middle, low = split3(own)
    packed = dot_nt(high, placing) + dot_nt(middle, placing) + dot_nt(low, placing)
    for ref in (up_ref, dn_ref):
        ref[ROWS : ROWS + GV, :] = packed
        ref[ROWS + GV :, :] = jnp.zeros((6, LANE), F32)


def y_shifted(q, plane, ylo, yhi, lane):
    plane = z_shift(plane, CZ[q], lane)
    if CY[q] == 1:
        k = YUP.index(q)
        return jnp.where(lane < Z, pltpu.roll(ylo, (LANE - k * Z) % LANE, 1), pltpu.roll(plane, Z, 1))
    if CY[q] == -1:
        k = YDN.index(q)
        return jnp.where(
            lane >= LANE - Z,
            pltpu.roll(yhi, (LANE - Z - k * Z) % LANE, 1),
            pltpu.roll(plane, LANE - Z, 1),
        )
    return plane


def second_kernel(col_ref, mine_ref, ylo_ref, yhi_ref, up_ref, dn_ref):
    lane = iota((8, LANE), 1)
    for ref, chosen, part, row in ((up_ref, XUP, 8, 7), (dn_ref, XDN, 0, 0)):
        ref[0:8, :] = jnp.zeros((8, LANE), F32)
        ylo = ylo_ref[part : part + 8, :]
        yhi = yhi_ref[part : part + 8, :]
        for k, q in enumerate(chosen):
            shifted = y_shifted(q, col_ref[q, part : part + 8, :], ylo, yhi, lane)
            ref[k : k + 1, :] = shifted[row : row + 1, :]
    grain_lane = iota((32, LANE), 1) // 8
    joined = jnp.where(
        one_of(grain_lane, (2, 4, 7)),
        ylo_ref[ROWS:, :],
        jnp.where(one_of(grain_lane, (0, 3, 5)), yhi_ref[ROWS:, :], mine_ref[ROWS:, :]),
    )
    up_ref[8:, :] = joined
    dn_ref[8:, :] = joined


def link_terms(cell, direction, picked, block_x, block_y):
    def component(table):
        plus = one_of(direction, [q for q in range(Q) if table[q] == 1])
        minus = one_of(direction, [q for q in range(Q) if table[q] == -1])
        return jnp.where(plus, 1.0, jnp.where(minus, -1.0, 0.0))

    step_x, step_y, step_z = component(CX), component(CY), component(CZ)
    scale = jnp.where(direction <= 6, W6_AXIS, W6_DIAG)
    rel_x = (block_x * E + cell // (E * Z)).astype(F32) + 0.5 * step_x - picked[0:1]
    rel_y = (block_y * E + cell // Z % E).astype(F32) + 0.5 * step_y - picked[1:2]
    rel_z = (cell % Z).astype(F32) + 0.5 * step_z - picked[2:3]
    wall_x = picked[3:4] + picked[7:8] * rel_z - picked[8:9] * rel_y
    wall_y = picked[4:5] + picked[8:9] * rel_x - picked[6:7] * rel_z
    wall_z = picked[5:6] + picked[6:7] * rel_y - picked[7:8] * rel_x
    return scale * (step_x * wall_x + step_y * wall_y + step_z * wall_z)


def third_kernel(
    place_ref, owner_ref, col_ref, ylo_ref, yhi_ref, mine_ref, xlo_ref, xhi_ref, grains_ref, moves_ref,
    link_ref, send_ref, table_ref, final_ref, block_ref,
):
    lane = iota((ROWS, LANE), 1)
    row = iota((ROWS, LANE), 0)
    grain_lane = iota((32, LANE), 1) // 8
    arrived = jnp.where(
        one_of(grain_lane, (5, 6, 7)),
        xlo_ref[8:, :],
        jnp.where(one_of(grain_lane, (0, 1, 2)), xhi_ref[8:, :], mine_ref[8:, :]),
    )
    own = grains_ref[:, 0, :]
    kept = jnp.where(moves_ref[...] == 4, own, 0.0)
    table_ref[:, 0, 0:256] = kept
    table_ref[:, 0, 256:320] = arrived[0:GV, 0:64]
    kept_parts = jnp.concatenate(split3(kept[0:16]), axis=0)
    arrived_parts = jnp.concatenate(split3(arrived[0:16]), axis=0)
    corrections = []
    directions = []
    for bx in range(2):
        cell = link_ref[0, bx : bx + 1, :]
        direction = link_ref[1, bx : bx + 1, :]
        slot = link_ref[2, bx : bx + 1, :]
        links = cell.shape[1]
        pick_kept = (iota((256, links), 0) == slot).astype(F32).astype(BF16)
        pick_arrived = (iota((LANE, links), 0) + 256 == slot).astype(F32).astype(BF16)
        picked = dot_nn(kept_parts, pick_kept) + dot_nn(arrived_parts, pick_arrived)
        picked = picked[0:16] + picked[16:32] + picked[32:48]
        side = iota((1, links), 1) // 256
        correction = link_terms(cell, direction, picked, place_ref[0] * 2 + bx, place_ref[1] * 2 + side)
        at_row = iota((8, links), 0) == cell // 64
        values = [part.astype(F32) for part in split3(correction)] + [direction.astype(F32)]
        left = jnp.concatenate([jnp.where(at_row, value, 0.0) for value in values], axis=0).astype(BF16)
        right = (iota((LANE, links), 0) == side * 64 + cell % 64).astype(F32).astype(BF16)
        dense = dot_nt(left, right)
        corrections.append(dense[0:8] + dense[8:16] + dense[16:24])
        directions.append(dense[24:32])
    correction = jnp.concatenate(corrections, axis=0)
    direction = jnp.concatenate(directions, axis=0).astype(I32)
    ylo = ylo_ref[0:ROWS, :]
    yhi = yhi_ref[0:ROWS, :]
    for q in range(Q):
        plane = y_shifted(q, col_ref[q], ylo, yhi, lane)
        if CX[q] == 1:
            k = XUP.index(q)
            plane = jnp.where(row == 0, xlo_ref[k : k + 1, :], pltpu.roll(plane, 1, 0))
        elif CX[q] == -1:
            k = XDN.index(q)
            plane = jnp.where(row == ROWS - 1, xhi_ref[k : k + 1, :], pltpu.roll(plane, ROWS - 1, 0))
        if q:
            plane = jnp.where(direction == OPP[q], col_ref[OPP[q]] - correction, plane)
        final_ref[q] = plane
    low_half = iota((8, LANE), 1) < 64
    for q in range(Q):
        even = final_ref[q, pl.ds(0, 8, stride=2), :]
        odd = final_ref[q, pl.ds(1, 8, stride=2), :]
        first = jnp.where(low_half, even, pltpu.roll(odd, 64, 1))
        second = jnp.where(low_half, pltpu.roll(even, 64, 1), odd)
        for bx in range(2):
            block_ref[bx * 2, 4 * q : 4 * q + 4, :] = first[4 * bx : 4 * bx + 4]
            block_ref[bx * 2 + 1, 4 * q : 4 * q + 4, :] = second[4 * bx : 4 * bx + 4]
    send_ref[...] = jnp.zeros(send_ref.shape, F32)
    for n in range(4):
        send_ref[owner_ref[n // 2, n % 2]] = block_ref[n]


def last_kernel(got_ref, out_ref):
    for slot in range(got_ref.shape[0]):
        out_ref[76 * slot : 76 * slot + 76, :] = got_ref[slot]


VMEM = pl.BlockSpec(memory_space=pltpu.VMEM)
SMEM = pl.BlockSpec(memory_space=pltpu.SMEM)


def ring(axis, step):
    count = lax.axis_size(axis)
    return [(i, (i + step) % count) for i in range(count)]


def body(pdf, grains, grain_moves, owner_map, link_lists):
    group = lax.axis_size("gx")
    place = jnp.stack([lax.axis_index("gx"), lax.axis_index("gy")]).astype(I32)

    def shape(*dims):
        return jax.ShapeDtypeStruct(dims, F32)

    col, y_up, y_dn = pl.pallas_call(
        first_kernel,
        out_shape=(shape(Q, ROWS, LANE), shape(48, LANE), shape(48, LANE)),
        in_specs=[VMEM] * 3,
        out_specs=(VMEM,) * 3,
        name="collide_pack",
    )(pdf, grains, grain_moves)
    ylo = lax.ppermute(y_up, "gy", ring("gy", 1))
    yhi = lax.ppermute(y_dn, "gy", ring("gy", -1))
    x_up, x_dn = pl.pallas_call(
        second_kernel,
        out_shape=(shape(40, LANE), shape(40, LANE)),
        in_specs=[VMEM] * 4,
        out_specs=(VMEM,) * 2,
        name="x_messages",
    )(col, y_up, ylo, yhi)
    xlo = lax.ppermute(x_up, "gx", ring("gx", 1))
    xhi = lax.ppermute(x_dn, "gx", ring("gx", -1))
    send, table = pl.pallas_call(
        third_kernel,
        out_shape=(shape(group, 76, LANE), shape(GV, 1, 320)),
        in_specs=[SMEM, SMEM] + [VMEM] * 9,
        out_specs=(VMEM,) * 2,
        scratch_shapes=[pltpu.VMEM((Q, ROWS, LANE), F32), pltpu.VMEM((4, 76, LANE), F32)],
        name="finish_blocks",
    )(place, owner_map, col, ylo, yhi, x_up, xlo, xhi, grains, grain_moves, link_lists)
    got = lax.all_to_all(send, "gx", split_axis=0, concat_axis=0, tiled=True)
    out = pl.pallas_call(
        last_kernel,
        out_shape=shape(group * 76, LANE),
        in_specs=[VMEM],
        out_specs=VMEM,
        name="lay_out",
    )(got)
    return (out.reshape(group, 1, Q, 512), table)


def solution(mesh):
    in_specs = (
        P(None, "gx", "gy"),
        P(None, "gx", "gy"),
        P("gx", "gy"),
        P("gx", "gy"),
        P(None, "gx", "gy"),
    )
    out_specs = (P("gx", "gy", None, None), P(None, "gx", "gy"))
    return jax.shard_map(body, mesh=mesh, in_specs=in_specs, out_specs=out_specs, check_vma=False)
```

time: 442 us -> 85.8 us (0.19)
  the two profiles are of different devices: /device:TPU:71 before, /device:TPU:64 now
where the time goes in v1:
time: 85.8 us; the launch traced here: 85.4 us
  blocking collectives  38 us (44%)
  starting transfers between devices  19.9 us (23%)
  waiting for transfers between devices  16.9 us (20%)
  Pallas kernels  8.09 us (9%)
  local copies, waits for them, and re-layouts  1.23 us (1%)
    all_to_all x1, blocking collectives, body(): got = lax.all_to_all(send, 'gx', split_axis=0, concat_axis=0, tiled=True)  38 us
    ppermute x1, waiting for transfers between devices, body(): xlo = lax.ppermute(x_up, 'gx', ring('gx', 1))  10.1 us
    ppermute x1, starting transfers between devices, body(): xhi = lax.ppermute(x_dn, 'gx', ring('gx', -1))  9.11 us
    ppermute x1, starting transfers between devices, body(): yhi = lax.ppermute(y_dn, 'gy', ring('gy', -1))  7 us
    ppermute x1, waiting for transfers between devices, body(): ylo = lax.ppermute(y_up, 'gy', ring('gy', 1))  6.72 us
    pallas_call x1, Pallas kernels, body(): pl.pallas_call(third_kernel, out_shape=(shape(group, 76, LANE), shape(GV,...  2.54 us
    pallas_call x1, Pallas kernels, body(): pl.pallas_call(first_kernel, out_shape=(shape(Q, ROWS, LANE), shape(48, L...  1.97 us
    pallas_call x1, Pallas kernels, body(): pl.pallas_call(last_kernel, out_shape=shape(group * 76, LANE), in_specs=[...  1.95 us
  transfers between devices with their start and end apart: 4, of which 2 were waited for; matrix products, arithmetic and copies ran while one was open for 1% of the time, Pallas kernels for 0%

profile of v1, /device:TPU:64, one launch (start us, length us, event | category | flops | bytes accessed | tf_op | source)
XLA Modules:
  0.0 85.4 jit_solution(16038709649910833225)
XLA Ops:
  0.6 2.0 %collide_pack.1 = (f32[19,16,128]{2,1,0:T(8,128)}, f32[48,128]{1,0:T(8,128)}, f32[48,128]{1,0:T(8,128)}) custom-call(f32[19,16,128]{2,1,0:T(8,128)} %pdf_ref.1, f32[26,1,256]{2,1,0:T(1,128)} %grains_ref.3, s32[1,256]{1,0:T(1,128)} %moves_ref.3), custom_call_target="tpu_custom_call" | custom-call | tf_op jit(solution)/shard_map/collide_pack/pallas_call | solution.py:281
  2.6 7.0 %collective-permute-start.1 = (f32[48,128]{1,0:T(8,128)}, f32[48,128]{1,0:T(8,128)S(1)}, u32[]{:S(2)}, u32[]{:S(2)}) collective-permute-start(f32[48,128]{1,0:T(8,128)} %get-tuple-element.11), channel_id=1, source_target_pairs={{0,63},{1,0},{2,1},{3,2},{4,3},{5,4},{6,5},{7,6},{8,7},{9,8},{10,9... | collective-permute-start | bytes 73736 | tf_op jit(solution)/shard_map/ppermute | solution.py:289
  9.6 1.9 %collective-permute-start = (f32[48,128]{1,0:T(8,128)}, f32[48,128]{1,0:T(8,128)S(1)}, u32[]{:S(2)}, u32[]{:S(2)}) collective-permute-start(f32[48,128]{1,0:T(8,128)} %get-tuple-element.10.mine_ref), channel_id=1, source_target_pairs={{0,1},{1,2},{2,3},{3,4},{4,5},{5,6},{6,7},{7,8},{8,9},{9,10},{10,1... | collective-permute-start | bytes 73736 | tf_op jit(solution)/shard_map/ppermute | solution.py:288
  11.5 0.0 collective-permute-done.1.yhi_ref
  11.5 0.0 copy-start
  11.6 6.7 %collective-permute-done.ylo_ref = f32[48,128]{1,0:T(8,128)S(1)} collective-permute-done((f32[48,128]{1,0:T(8,128)}, f32[48,128]{1,0:T(8,128)S(1)}, u32[]{:S(2)}, u32[]{:S(2)}) %collective-permute-start) | collective-permute-done | bytes 24608 | tf_op jit(solution)/shard_map/ppermute | solution.py:288
  18.3 0.0 copy-start.1
  18.3 0.0 copy-done
  18.3 0.6 copy-done.1
  18.9 1.6 %x_messages.1 = (f32[40,128]{1,0:T(8,128)}, f32[40,128]{1,0:T(8,128)}) custom-call(f32[19,16,128]{2,1,0:T(8,128)} %get-tuple-element.9.col_ref, f32[48,128]{1,0:T(8,128)} %get-tuple-element.10.mine_ref, f32[48,128]{1,0:T(8,128)} %copy-done.1, f32[48,128]{1,0:T(8,128)} %copy-done), custom_call_target="tpu_custom_call" | custom-call | tf_op jit(solution)/shard_map/x_messages/pallas_call | solution.py:290
  20.5 9.1 %collective-permute-start.3 = (f32[40,128]{1,0:T(8,128)}, f32[40,128]{1,0:T(8,128)S(1)}, u32[]{:S(2)}, u32[]{:S(2)}) collective-permute-start(f32[40,128]{1,0:T(8,128)} %get-tuple-element.13), channel_id=1, source_target_pairs={{0,960},{64,0},{128,64},{192,128},{256,192},{320,256},{384,320},{4... | collective-permute-start | bytes 61448 | tf_op jit(solution)/shard_map/ppermute | solution.py:298
  29.6 1.9 %collective-permute-start.2 = (f32[40,128]{1,0:T(8,128)}, f32[40,128]{1,0:T(8,128)S(1)}, u32[]{:S(2)}, u32[]{:S(2)}) collective-permute-start(f32[40,128]{1,0:T(8,128)} %get-tuple-element.12.mine_ref), channel_id=1, source_target_pairs={{0,64},{64,128},{128,192},{192,256},{256,320},{320,384},{384,448},... | collective-permute-start | bytes 61448 | tf_op jit(solution)/shard_map/ppermute | solution.py:297
  31.6 0.6 pad_add_fusion.place_ref
  32.1 0.0 collective-permute-done.3.xhi_ref
  32.1 0.0 copy-start.2
  32.1 10.1 %collective-permute-done.2.xlo_ref = f32[40,128]{1,0:T(8,128)S(1)} collective-permute-done((f32[40,128]{1,0:T(8,128)}, f32[40,128]{1,0:T(8,128)S(1)}, u32[]{:S(2)}, u32[]{:S(2)}) %collective-permute-start.2) | collective-permute-done | bytes 20512 | tf_op jit(solution)/shard_map/ppermute | solution.py:297
  42.3 0.0 copy-done.2
  42.3 0.0 copy-start.3
  42.3 0.6 copy-done.3
  42.9 2.5 %finish_blocks.1 = (f32[16,76,128]{2,1,0:T(8,128)}, f32[26,1,320]{2,1,0:T(1,128)}) custom-call(s32[2]{0:T(128)} %pad_add_fusion.place_ref, s32[2,2]{1,0:T(2,128)} %owner_ref.1, f32[19,16,128]{2,1,0:T(8,128)} %get-tuple-element.9.col_ref, f32[48,128]{1,0:T(8,128)} %copy-done.1, f32[48,128]{1,0:T(8,128)} %copy-done, f32[40,128]{1,0:T(8,128)} %get-tuple-element.12.mine_ref, ...), custom_call_target="tpu_custom_call" | custom-call | tf_op jit(solution)/shard_map/finish_blocks/pallas_call | solution.py:299
  45.4 38.0 %all_to_all.5.got_ref = f32[16,76,128]{2,1,0:T(8,128)} all-to-all(f32[16,76,128]{2,1,0:T(8,128)} %get-tuple-element.14), channel_id=1, replica_groups=mesh['gx'=16,'gy'=64] {'gx'}, dimensions={0} | all-to-all | bytes 1245184 | tf_op jit(solution)/shard_map/all_to_all | solution.py:307
  83.4 2.0 %lay_out.1 = f32[1216,128]{1,0:T(8,128)} custom-call(f32[16,76,128]{2,1,0:T(8,128)} %all_to_all.5.got_ref), custom_call_target="tpu_custom_call" | custom-call | tf_op jit(solution)/shard_map/lay_out/pallas_call | solution.py:308
Async XLA Ops:
  2.6 8.9 %collective-permute-start.1 = (f32[48,128]{1,0:T(8,128)}, f32[48,128]{1,0:T(8,128)S(1)}, u32[]{:S(2)}, u32[]{:S(2)}) collective-permute-start(f32[48,128]{1,0:T(8,128)} %get-tuple-element.11), channel_id=1, source_target_pairs={{0,63},{1,0},{2,1},{3,2},{4,3},{5,4},{6,5},{7,6},{8,7},{9,8},{10,9... | collective-permute-start | bytes 73736 | tf_op jit(solution)/shard_map/ppermute | solution.py:289
  9.6 8.7 %collective-permute-start = (f32[48,128]{1,0:T(8,128)}, f32[48,128]{1,0:T(8,128)S(1)}, u32[]{:S(2)}, u32[]{:S(2)}) collective-permute-start(f32[48,128]{1,0:T(8,128)} %get-tuple-element.10.mine_ref), channel_id=1, source_target_pairs={{0,1},{1,2},{2,3},{3,4},{4,5},{5,6},{6,7},{7,8},{8,9},{9,10},{10,1... | collective-permute-start | bytes 73736 | tf_op jit(solution)/shard_map/ppermute | solution.py:288
  11.5 6.7 %copy-start = (f32[48,128]{1,0:T(8,128)}, f32[48,128]{1,0:T(8,128)S(1)}, u32[]{:S(2)}) copy-start(f32[48,128]{1,0:T(8,128)S(1)} %collective-permute-done.1.yhi_ref) | copy-start | bytes 73732
  18.3 0.6 copy-start.1
  20.5 11.6 %collective-permute-start.3 = (f32[40,128]{1,0:T(8,128)}, f32[40,128]{1,0:T(8,128)S(1)}, u32[]{:S(2)}, u32[]{:S(2)}) collective-permute-start(f32[40,128]{1,0:T(8,128)} %get-tuple-element.13), channel_id=1, source_target_pairs={{0,960},{64,0},{128,64},{192,128},{256,192},{320,256},{384,320},{4... | collective-permute-start | bytes 61448 | tf_op jit(solution)/shard_map/ppermute | solution.py:298
  29.6 12.6 %collective-permute-start.2 = (f32[40,128]{1,0:T(8,128)}, f32[40,128]{1,0:T(8,128)S(1)}, u32[]{:S(2)}, u32[]{:S(2)}) collective-permute-start(f32[40,128]{1,0:T(8,128)} %get-tuple-element.12.mine_ref), channel_id=1, source_target_pairs={{0,64},{64,128},{128,192},{192,256},{256,320},{320,384},{384,448},... | collective-permute-start | bytes 61448 | tf_op jit(solution)/shard_map/ppermute | solution.py:297
  32.1 10.1 %copy-start.2 = (f32[40,128]{1,0:T(8,128)}, f32[40,128]{1,0:T(8,128)S(1)}, u32[]{:S(2)}) copy-start(f32[40,128]{1,0:T(8,128)S(1)} %collective-permute-done.3.xhi_ref) | copy-start | bytes 61444
  42.3 0.6 copy-start.3

commit v2 on v1

--- a/solution.py
+++ b/solution.py
@@ -154,7 +154,8 @@
     return plane
 
 
-def second_kernel(col_ref, mine_ref, ylo_ref, yhi_ref, up_ref, dn_ref):
+def second_kernel(col_ref, mine_ref, ylo_ref, yhi_ref, after_ref, up_ref, dn_ref):
+    del after_ref
     lane = iota((8, LANE), 1)
     for ref, chosen, part, row in ((up_ref, XUP, 8, 7), (dn_ref, XDN, 0, 0)):
         ref[0:8, :] = jnp.zeros((8, LANE), F32)
@@ -173,93 +174,142 @@
     dn_ref[8:, :] = joined
 
 
-def link_terms(cell, direction, picked, block_x, block_y):
-    def component(table):
-        plus = one_of(direction, [q for q in range(Q) if table[q] == 1])
-        minus = one_of(direction, [q for q in range(Q) if table[q] == -1])
-        return jnp.where(plus, 1.0, jnp.where(minus, -1.0, 0.0))
-
-    step_x, step_y, step_z = component(CX), component(CY), component(CZ)
-    scale = jnp.where(direction <= 6, W6_AXIS, W6_DIAG)
-    rel_x = (block_x * E + cell // (E * Z)).astype(F32) + 0.5 * step_x - picked[0:1]
-    rel_y = (block_y * E + cell // Z % E).astype(F32) + 0.5 * step_y - picked[1:2]
-    rel_z = (cell % Z).astype(F32) + 0.5 * step_z - picked[2:3]
-    wall_x = picked[3:4] + picked[7:8] * rel_z - picked[8:9] * rel_y
-    wall_y = picked[4:5] + picked[8:9] * rel_x - picked[6:7] * rel_z
-    wall_z = picked[5:6] + picked[6:7] * rel_y - picked[7:8] * rel_x
-    return scale * (step_x * wall_x + step_y * wall_y + step_z * wall_z)
-
-
-def third_kernel(
-    place_ref, owner_ref, col_ref, ylo_ref, yhi_ref, mine_ref, xlo_ref, xhi_ref, grains_ref, moves_ref,
-    link_ref, send_ref, table_ref, final_ref, block_ref,
+def link_kernel(place_x_ref, place_y_ref, link_ref, after_ref, kept_ref, arrived_ref, spread_ref, term_ref, dense_ref):
+    del after_ref
+    for bx in range(2):
+        cell = link_ref[0, bx : bx + 1, :]
+        direction = link_ref[1, bx : bx + 1, :]
+        slot = link_ref[2, bx : bx + 1, :]
+        links = cell.shape[1]
+        side = iota((1, links), 1) // 256
+
+        def component(table):
+            plus = one_of(direction, [q for q in range(Q) if table[q] == 1])
+            minus = one_of(direction, [q for q in range(Q) if table[q] == -1])
+            return jnp.where(plus, 1.0, jnp.where(minus, -1.0, 0.0))
+
+        steps = [component(table) for table in (CX, CY, CZ)]
+        corner = (
+            (place_x_ref[0] * 2 + bx) * E + cell // (E * Z),
+            (place_y_ref[0] * 2 + side) * E + cell // Z % E,
+            cell % Z,
+        )
+        row = cell // (E * Z)
+        terms = [c.astype(F32) + 0.5 * step for c, step in zip(corner, steps)] + steps
+        terms += [jnp.where(direction <= 6, W6_AXIS, W6_DIAG), row.astype(F32)]
+        for k, term in enumerate(terms):
+            term_ref[bx, k : k + 1, :] = term
+        kept_ref[bx] = (iota((256, links), 0) == slot).astype(F32).astype(BF16)
+        arrived_ref[bx] = (iota((LANE, links), 0) + 256 == slot).astype(F32).astype(BF16)
+        spread = (iota((LANE, links), 0) == side * 64 + cell % 64).astype(F32).astype(BF16)
+        spread_ref[bx] = spread
+        left = jnp.where(iota((8, links), 0) == row, direction.astype(F32), 0.0).astype(BF16)
+        dense_ref[8 * bx : 8 * bx + 8, :] = dot_nt(left, spread)
+
+
+def block_order(scratch_ref, plane):
+    low_half = iota((8, LANE), 1) < 64
+    scratch_ref[...] = plane
+    even = scratch_ref[pl.ds(0, 8, stride=2), :]
+    odd = scratch_ref[pl.ds(1, 8, stride=2), :]
+    first = jnp.where(low_half, even, pltpu.roll(odd, 64, 1))
+    second = jnp.where(low_half, pltpu.roll(even, 64, 1), odd)
+    return first, second
+
+
+def shift_kernel(
+    col_ref, ylo_ref, yhi_ref, mine_ref, grains_ref, moves_ref, kept_ref, arrived_ref, dense_ref, after_ref,
+    plane_ref, value_ref, toward_ref, pick_ref, own_ref, scratch_ref,
 ):
+    del after_ref
     lane = iota((ROWS, LANE), 1)
-    row = iota((ROWS, LANE), 0)
+    ylo = ylo_ref[0:ROWS, :]
+    yhi = yhi_ref[0:ROWS, :]
+    for q in range(Q):
+        plane = y_shifted(q, col_ref[q], ylo, yhi, lane)
+        if CX[q]:
+            plane = pltpu.roll(plane, CX[q] % ROWS, 0)
+        for ref, given in ((plane_ref, plane), (value_ref, col_ref[OPP[q]])):
+            for half, part in enumerate(block_order(scratch_ref.at[q % 4 + (4 if ref is value_ref else 0)], given)):
+                ref[q, half] = part
+    for half, part in enumerate(block_order(scratch_ref.at[0], dense_ref[...])):
+        toward_ref[half] = part.astype(I32)
+    kept = jnp.where(moves_ref[...] == 4, grains_ref[:, 0, :], 0.0)
+    own_ref[...] = kept
+    stay = one_of(iota((32, LANE), 1) // 8, (3, 4))
+    arrived = jnp.where(stay, mine_ref[8:, :], 0.0)
+    kept_parts = jnp.concatenate(split3(kept[0:16]), axis=0)
+    arrived_parts = jnp.concatenate(split3(arrived[0:16]), axis=0)
+    for bx in range(2):
+        picked = dot_nn(kept_parts, kept_ref[bx]) + dot_nn(arrived_parts, arrived_ref[bx])
+        pick_ref[bx] = picked[0:16] + picked[16:32] + picked[32:48]
+
+
+def table_kernel(mine_ref, xlo_ref, xhi_ref, own_ref, table_ref):
     grain_lane = iota((32, LANE), 1) // 8
     arrived = jnp.where(
         one_of(grain_lane, (5, 6, 7)),
         xlo_ref[8:, :],
         jnp.where(one_of(grain_lane, (0, 1, 2)), xhi_ref[8:, :], mine_ref[8:, :]),
     )
-    own = grains_ref[:, 0, :]
-    kept = jnp.where(moves_ref[...] == 4, own, 0.0)
-    table_ref[:, 0, 0:256] = kept
+    table_ref[:, 0, 0:256] = own_ref[...]
     table_ref[:, 0, 256:320] = arrived[0:GV, 0:64]
-    kept_parts = jnp.concatenate(split3(kept[0:16]), axis=0)
-    arrived_parts = jnp.concatenate(split3(arrived[0:16]), axis=0)
+
+
+def finish_kernel(
+    owner_ref, plane_ref, value_ref, toward_ref, xlo_ref, xhi_ref, pick_ref,
+    arrived_ref, spread_ref, term_ref, send_ref, scratch_ref,
+):
+    send_ref[...] = jnp.zeros(send_ref.shape, F32)
+    grain_lane = iota((16, LANE), 1) // 8
+    moved = jnp.where(
+        one_of(grain_lane, (5, 6, 7)),
+        xlo_ref[8:24, :],
+        jnp.where(one_of(grain_lane, (0, 1, 2)), xhi_ref[8:24, :], 0.0),
+    )
+    moved_parts = jnp.concatenate(split3(moved), axis=0)
     corrections = []
-    directions = []
     for bx in range(2):
-        cell = link_ref[0, bx : bx + 1, :]
-        direction = link_ref[1, bx : bx + 1, :]
-        slot = link_ref[2, bx : bx + 1, :]
-        links = cell.shape[1]
-        pick_kept = (iota((256, links), 0) == slot).astype(F32).astype(BF16)
-        pick_arrived = (iota((LANE, links), 0) + 256 == slot).astype(F32).astype(BF16)
-        picked = dot_nn(kept_parts, pick_kept) + dot_nn(arrived_parts, pick_arrived)
-        picked = picked[0:16] + picked[16:32] + picked[32:48]
-        side = iota((1, links), 1) // 256
-        correction = link_terms(cell, direction, picked, place_ref[0] * 2 + bx, place_ref[1] * 2 + side)
-        at_row = iota((8, links), 0) == cell // 64
-        values = [part.astype(F32) for part in split3(correction)] + [direction.astype(F32)]
-        left = jnp.concatenate([jnp.where(at_row, value, 0.0) for value in values], axis=0).astype(BF16)
-        right = (iota((LANE, links), 0) == side * 64 + cell % 64).astype(F32).astype(BF16)
-        dense = dot_nt(left, right)
+        picked = dot_nn(moved_parts, arrived_ref[bx])
+        g = pick_ref[bx] + (picked[0:16] + picked[16:32] + picked[32:48])
+        mid_x, mid_y, mid_z, step_x, step_y, step_z, scale, at = (term_ref[bx, k : k + 1, :] for k in range(8))
+        rel_x = mid_x - g[0:1]
+        rel_y = mid_y - g[1:2]
+        rel_z = mid_z - g[2:3]
+        wall_x = g[3:4] + g[7:8] * rel_z - g[8:9] * rel_y
+        wall_y = g[4:5] + g[8:9] * rel_x - g[6:7] * rel_z
+        wall_z = g[5:6] + g[6:7] * rel_y - g[7:8] * rel_x
+        correction = scale * (step_x * wall_x + step_y * wall_y + step_z * wall_z)
+        here = iota((8, correction.shape[1]), 0) == at.astype(I32)
+        left = jnp.concatenate(
+            [jnp.where(here, part.astype(F32), 0.0) for part in split3(correction)], axis=0
+        ).astype(BF16)
+        dense = dot_nt(left, spread_ref[bx])
         corrections.append(dense[0:8] + dense[8:16] + dense[16:24])
-        directions.append(dense[24:32])
     correction = jnp.concatenate(corrections, axis=0)
-    direction = jnp.concatenate(directions, axis=0).astype(I32)
-    ylo = ylo_ref[0:ROWS, :]
-    yhi = yhi_ref[0:ROWS, :]
+    correction = block_order(scratch_ref, correction)
+    base = [owner_ref[n // 2, n % 2] * Q for n in range(4)]
+    low_half = iota((8, LANE), 1) < 64
+    row = iota((8, LANE), 0)
+    first_row = jnp.logical_and(row == 0, low_half)
+    last_row = jnp.logical_and(row == 7, jnp.logical_not(low_half))
+    turned_low = pltpu.roll(xlo_ref[0:8, :], 64, 1)
+    turned_high = pltpu.roll(xhi_ref[0:8, :], 64, 1)
     for q in range(Q):
-        plane = y_shifted(q, col_ref[q], ylo, yhi, lane)
-        if CX[q] == 1:
-            k = XUP.index(q)
-            plane = jnp.where(row == 0, xlo_ref[k : k + 1, :], pltpu.roll(plane, 1, 0))
-        elif CX[q] == -1:
-            k = XDN.index(q)
-            plane = jnp.where(row == ROWS - 1, xhi_ref[k : k + 1, :], pltpu.roll(plane, ROWS - 1, 0))
-        if q:
-            plane = jnp.where(direction == OPP[q], col_ref[OPP[q]] - correction, plane)
-        final_ref[q] = plane
-    low_half = iota((8, LANE), 1) < 64
-    for q in range(Q):
-        even = final_ref[q, pl.ds(0, 8, stride=2), :]
-        odd = final_ref[q, pl.ds(1, 8, stride=2), :]
-        first = jnp.where(low_half, even, pltpu.roll(odd, 64, 1))
-        second = jnp.where(low_half, pltpu.roll(even, 64, 1), odd)
-        for bx in range(2):
-            block_ref[bx * 2, 4 * q : 4 * q + 4, :] = first[4 * bx : 4 * bx + 4]
-            block_ref[bx * 2 + 1, 4 * q : 4 * q + 4, :] = second[4 * bx : 4 * bx + 4]
-    send_ref[...] = jnp.zeros(send_ref.shape, F32)
-    for n in range(4):
-        send_ref[owner_ref[n // 2, n % 2]] = block_ref[n]
-
-
-def last_kernel(got_ref, out_ref):
-    for slot in range(got_ref.shape[0]):
-        out_ref[76 * slot : 76 * slot + 76, :] = got_ref[slot]
+        for half in range(2):
+            part = plane_ref[q, half]
+            if CX[q] == 1:
+                k = XUP.index(q)
+                edge = turned_low[k : k + 1] if half else xlo_ref[k : k + 1, :]
+                part = jnp.where(first_row, edge, part)
+            elif CX[q] == -1:
+                k = XDN.index(q)
+                edge = xhi_ref[k : k + 1, :] if half else turned_high[k : k + 1]
+                part = jnp.where(last_row, edge, part)
+            if q:
+                part = jnp.where(toward_ref[half] == OPP[q], value_ref[q, half] - correction[half], part)
+            send_ref[base[half] + q] = part[0:4]
+            send_ref[base[2 + half] + q] = part[4:8]
 
 
 VMEM = pl.BlockSpec(memory_space=pltpu.VMEM)
@@ -271,48 +321,83 @@
     return [(i, (i + step) % count) for i in range(count)]
 
 
+def near(*arrays):
+    return tuple(pltpu.with_memory_space_constraint(a, pltpu.VMEM) for a in arrays)
+
+
+def chip(*dims, dtype=F32):
+    return pltpu.VMEM(dims, dtype)
+
+
 def body(pdf, grains, grain_moves, owner_map, link_lists):
     group = lax.axis_size("gx")
-    place = jnp.stack([lax.axis_index("gx"), lax.axis_index("gy")]).astype(I32)
-
-    def shape(*dims):
-        return jax.ShapeDtypeStruct(dims, F32)
-
+    place_x = lax.axis_index("gx").astype(I32).reshape(1)
+    place_y = lax.axis_index("gy").astype(I32).reshape(1)
+    links = link_lists.shape[2]
     col, y_up, y_dn = pl.pallas_call(
         first_kernel,
-        out_shape=(shape(Q, ROWS, LANE), shape(48, LANE), shape(48, LANE)),
+        out_shape=(chip(Q, ROWS, LANE), chip(48, LANE), chip(48, LANE)),
         in_specs=[VMEM] * 3,
         out_specs=(VMEM,) * 3,
         name="collide_pack",
     )(pdf, grains, grain_moves)
     ylo = lax.ppermute(y_up, "gy", ring("gy", 1))
     yhi = lax.ppermute(y_dn, "gy", ring("gy", -1))
+    kept, arrived, spread, terms, dense = pl.pallas_call(
+        link_kernel,
+        out_shape=(
+            chip(2, 256, links, dtype=BF16),
+            chip(2, LANE, links, dtype=BF16),
+            chip(2, LANE, links, dtype=BF16),
+            chip(2, 8, links),
+            chip(ROWS, LANE),
+        ),
+        in_specs=[SMEM, SMEM, VMEM, VMEM],
+        out_specs=(VMEM,) * 5,
+        cost_estimate=pl.CostEstimate(flops=4_000_000, bytes_accessed=1_000_000, transcendentals=0),
+        name="link_maps",
+    )(place_x, place_y, link_lists, *near(y_up))
     x_up, x_dn = pl.pallas_call(
         second_kernel,
-        out_shape=(shape(40, LANE), shape(40, LANE)),
-        in_specs=[VMEM] * 4,
+        out_shape=(chip(40, LANE), chip(40, LANE)),
+        in_specs=[VMEM] * 5,
         out_specs=(VMEM,) * 2,
         name="x_messages",
-    )(col, y_up, ylo, yhi)
+    )(*near(col, y_up, ylo, yhi, terms))
     xlo = lax.ppermute(x_up, "gx", ring("gx", 1))
     xhi = lax.ppermute(x_dn, "gx", ring("gx", -1))
-    send, table = pl.pallas_call(
-        third_kernel,
-        out_shape=(shape(group, 76, LANE), shape(GV, 1, 320)),
-        in_specs=[SMEM, SMEM] + [VMEM] * 9,
-        out_specs=(VMEM,) * 2,
-        scratch_shapes=[pltpu.VMEM((Q, ROWS, LANE), F32), pltpu.VMEM((4, 76, LANE), F32)],
+    plane, value, toward, pick, own = pl.pallas_call(
+        shift_kernel,
+        out_shape=(
+            chip(Q, 2, 8, LANE),
+            chip(Q, 2, 8, LANE),
+            chip(2, 8, LANE, dtype=I32),
+            chip(2, 16, links),
+            chip(GV, 256),
+        ),
+        in_specs=[VMEM] * 10,
+        out_specs=(VMEM,) * 5,
+        scratch_shapes=[pltpu.VMEM((8, ROWS, LANE), F32)],
+        cost_estimate=pl.CostEstimate(flops=4_000_000, bytes_accessed=1_000_000, transcendentals=0),
+        name="shift_planes",
+    )(*near(col, ylo, yhi, x_up), grains, grain_moves, *near(kept, arrived, dense, x_dn))
+    send = pl.pallas_call(
+        finish_kernel,
+        out_shape=jax.ShapeDtypeStruct((group * Q, 4, LANE), F32),
+        in_specs=[SMEM] + [VMEM] * 9,
+        out_specs=VMEM,
+        scratch_shapes=[pltpu.VMEM((ROWS, LANE), F32)],
         name="finish_blocks",
-    )(place, owner_map, col, ylo, yhi, x_up, xlo, xhi, grains, grain_moves, link_lists)
-    got = lax.all_to_all(send, "gx", split_axis=0, concat_axis=0, tiled=True)
-    out = pl.pallas_call(
-        last_kernel,
-        out_shape=shape(group * 76, LANE),
-        in_specs=[VMEM],
+    )(owner_map, *near(plane, value, toward, xlo, xhi, pick, arrived, spread, terms))
+    table = pl.pallas_call(
+        table_kernel,
+        out_shape=jax.ShapeDtypeStruct((GV, 1, 320), F32),
+        in_specs=[VMEM] * 4,
         out_specs=VMEM,
-        name="lay_out",
-    )(got)
-    return (out.reshape(group, 1, Q, 512), table)
+        name="grain_table",
+    )(*near(x_up, xlo, xhi, own))
+    out = lax.all_to_all(send.reshape(group, 1, Q, 512), "gx", split_axis=0, concat_axis=0, tiled=True)
+    return (out, table)
 
 
 def solution(mesh):

time: 85.8 us -> 75.6 us (0.88)
  the two profiles are of different devices: /device:TPU:64 before, /device:TPU:31 now
where the time goes in v2:
time: 75.6 us; the launch traced here: 75.1 us
  waiting for transfers between devices  35 us (46%)
  starting transfers between devices  32.3 us (43%)
  Pallas kernels  6.32 us (8%)
  local copies, waits for them, and re-layouts  0.83 us (1%)
    all_to_all x1, waiting for transfers between devices, body(): lax.all_to_all(send.reshape(group, 1, Q, 512), 'gx', split_axis=0, concat...  32.3 us
    ppermute x1, starting transfers between devices, body(): xhi = lax.ppermute(x_dn, 'gx', ring('gx', -1))  17.9 us
    ppermute x1, starting transfers between devices, body(): ylo = lax.ppermute(y_up, 'gy', ring('gy', 1))  6.3 us
    all_to_all x1, starting transfers between devices, body(): lax.all_to_all(send.reshape(group, 1, Q, 512), 'gx', split_axis=0, concat...  3.59 us
    ppermute x1, waiting for transfers between devices, body(): xlo = lax.ppermute(x_up, 'gx', ring('gx', 1))  2.66 us
    ppermute x1, starting transfers between devices, body(): yhi = lax.ppermute(y_dn, 'gy', ring('gy', -1))  2.58 us
    pallas_call x1, Pallas kernels, body(): pl.pallas_call(finish_kernel, out_shape=jax.ShapeDtypeStruct((group * Q,...  2.02 us
    ppermute x1, starting transfers between devices, body(): xlo = lax.ppermute(x_up, 'gx', ring('gx', 1))  1.92 us
  transfers between devices with their start and end apart: 5, of which 2 were waited for; matrix products, arithmetic and copies ran while one was open for 0% of the time, Pallas kernels for 4%

profile of v2, /device:TPU:31, one launch (start us, length us, event | category | flops | bytes accessed | tf_op | source)
XLA Modules:
  0.0 75.1 jit_solution(16041984714382318822)
XLA Ops:
  0.6 1.3 %collide_pack.1 = (f32[19,16,128]{2,1,0:T(8,128)S(1)}, f32[48,128]{1,0:T(8,128)S(1)}, f32[48,128]{1,0:T(8,128)S(1)}) custom-call(f32[19,16,128]{2,1,0:T(8,128)} %pdf_ref.1, f32[26,1,256]{2,1,0:T(1,128)} %grains_ref.3, s32[1,256]{1,0:T(1,128)} %moves_ref.3), custom_call_target="tpu_custom_call" | custom-call | tf_op jit(solution)/shard_map/collide_pack/pallas_call | solution.py:337
  2.0 2.6 %collective-permute-start.1 = (f32[48,128]{1,0:T(8,128)S(1)}, f32[48,128]{1,0:T(8,128)S(1)}, u32[]{:S(2)}, u32[]{:S(2)}) collective-permute-start(f32[48,128]{1,0:T(8,128)S(1)} %get-tuple-element.19), channel_id=1, source_target_pairs={{0,63},{1,0},{2,1},{3,2},{4,3},{5,4},{6,5},{7,6},{8,7},{9,8},{10,9... | collective-permute-start | bytes 73736 | tf_op jit(solution)/shard_map/ppermute | solution.py:345
  4.6 6.3 %collective-permute-start = (f32[48,128]{1,0:T(8,128)S(1)}, f32[48,128]{1,0:T(8,128)S(1)}, u32[]{:S(2)}, u32[]{:S(2)}) collective-permute-start(f32[48,128]{1,0:T(8,128)S(1)} %get-tuple-element.18.after_ref.mine_ref), channel_id=1, source_target_pairs={{0,1},{1,2},{2,3},{3,4},{4,5},{5,6},{6,7},{7,8},{8,9},{9,10},{10,1... | collective-permute-start | bytes 73736 | tf_op jit(solution)/shard_map/ppermute | solution.py:344
  10.9 1.1 %link_maps.1 = (bf16[2,256,512]{2,1,0:T(8,128)(2,1)S(1)}, bf16[2,128,512]{2,1,0:T(8,128)(2,1)S(1)}, bf16[2,128,512]{2,1,0:T(8,128)(2,1)S(1)}, f32[2,8,512]{2,1,0:T(8,128)S(1)}, f32[16,128]{1,0:T(8,128)S(1)}) custom-call(s32[1]{0:T(128)} %bitcast.place_x_ref, s32[1]{0:T(128)} %bitcast.1.place_y_ref, s32[3,2,512]{2,1,0:T(2,128)} %link_ref.1, ...), custom_call_target="tpu_custom_call" | custom-call | flops 4000000 | bytes 1000000 | tf_op jit(solution)/shard_map/link_maps/pallas_call | solution.py:346
  12.0 0.0 collective-permute-done.1.yhi_ref
  12.0 0.0 collective-permute-done.ylo_ref
  12.0 0.1 x_messages.1
  12.1 17.9 %collective-permute-start.3 = (f32[40,128]{1,0:T(8,128)S(1)}, f32[40,128]{1,0:T(8,128)S(1)}, u32[]{:S(2)}, u32[]{:S(2)}) collective-permute-start(f32[40,128]{1,0:T(8,128)S(1)} %get-tuple-element.25.after_ref), channel_id=1, source_target_pairs={{0,960},{64,0},{128,64},{192,128},{256,192},{320,256},{384,320},{4... | collective-permute-start | bytes 61448 | tf_op jit(solution)/shard_map/ppermute | solution.py:368
  30.0 1.9 %collective-permute-start.2 = (f32[40,128]{1,0:T(8,128)S(1)}, f32[40,128]{1,0:T(8,128)S(1)}, u32[]{:S(2)}, u32[]{:S(2)}) collective-permute-start(f32[40,128]{1,0:T(8,128)S(1)} %get-tuple-element.21.mine_ref), channel_id=1, source_target_pairs={{0,64},{64,128},{128,192},{192,256},{256,320},{320,384},{384,448},... | collective-permute-start | bytes 61448 | tf_op jit(solution)/shard_map/ppermute | solution.py:367
  32.0 1.1 %shift_planes.1 = (f32[19,2,8,128]{3,2,1,0:T(8,128)S(1)}, f32[19,2,8,128]{3,2,1,0:T(8,128)S(1)}, s32[2,8,128]{2,1,0:T(8,128)S(1)}, f32[2,16,512]{2,1,0:T(8,128)S(1)}, f32[26,256]{1,0:T(8,128)S(1)}) custom-call(f32[19,16,128]{2,1,0:T(8,128)S(1)} %get-tuple-element.17.col_ref, f32[48,128]{1,0:T(8,128)S(1)} %collective-permute-done.ylo_ref, ...), custom_call_target="tpu_custom_call" | custom-call | flops 4000000 | bytes 1000000 | tf_op jit(solution)/shard_map/shift_planes/pallas_call | solution.py:369
  33.1 0.0 collective-permute-done.3.xhi_ref
  33.1 2.7 %collective-permute-done.2.xlo_ref = f32[40,128]{1,0:T(8,128)S(1)} collective-permute-done((f32[40,128]{1,0:T(8,128)S(1)}, f32[40,128]{1,0:T(8,128)S(1)}, u32[]{:S(2)}, u32[]{:S(2)}) %collective-permute-start.2) | collective-permute-done | bytes 20512 | tf_op jit(solution)/shard_map/ppermute | solution.py:367
  35.8 2.0 %finish_blocks.1 = f32[304,4,128]{2,1,0:T(4,128)} custom-call(s32[2,2]{1,0:T(2,128)} %owner_ref.1, f32[19,2,8,128]{3,2,1,0:T(8,128)S(1)} %get-tuple-element.26.plane_ref, f32[19,2,8,128]{3,2,1,0:T(8,128)S(1)} %get-tuple-element.27.value_ref, s32[2,8,128]{2,1,0:T(8,128)S(1)} %get-tuple-element.28.toward_ref, f32[40,128]{1,0:T(8,128)S(1)} %collective-permute-done.2.xlo_ref, ...), custom_call_target="tpu_custom_call" | custom-call | tf_op jit(solution)/shard_map/finish_blocks/pallas_call | solution.py:384
  37.8 3.6 %all-to-all-start = ((f32[16,1,19,512]{3,1,2,0:T(1,128)}), f32[16,1,19,512]{3,1,2,0:T(1,128)S(1)}, u32[]{:S(2)}, u32[]{:S(2)}) async-start(f32[16,1,19,512]{3,1,2,0:T(1,128)} %bitcast.3), calls=%async_computation | async-start | bytes 1245184 | tf_op jit(solution)/shard_map/all_to_all | solution.py:399
  41.4 0.6 grain_table.1
  42.0 32.3 %all-to-all-done = f32[16,1,19,512]{3,1,2,0:T(1,128)S(1)} async-done(((f32[16,1,19,512]{3,1,2,0:T(1,128)}), f32[16,1,19,512]{3,1,2,0:T(1,128)S(1)}, u32[]{:S(2)}, u32[]{:S(2)}) %all-to-all-start) | async-done | bytes 622624 | tf_op jit(solution)/shard_map/all_to_all | solution.py:399
  74.3 0.8 %copy.11 = f32[16,1,19,512]{3,1,2,0:T(1,128)} copy(f32[16,1,19,512]{3,1,2,0:T(1,128)S(1)} %all-to-all-done) | data formatting | bytes 1245184
Async XLA Ops:
  2.0 10.0 %collective-permute-start.1 = (f32[48,128]{1,0:T(8,128)S(1)}, f32[48,128]{1,0:T(8,128)S(1)}, u32[]{:S(2)}, u32[]{:S(2)}) collective-permute-start(f32[48,128]{1,0:T(8,128)S(1)} %get-tuple-element.19), channel_id=1, source_target_pairs={{0,63},{1,0},{2,1},{3,2},{4,3},{5,4},{6,5},{7,6},{8,7},{9,8},{10,9... | collective-permute-start | bytes 73736 | tf_op jit(solution)/shard_map/ppermute | solution.py:345
  4.6 7.4 %collective-permute-start = (f32[48,128]{1,0:T(8,128)S(1)}, f32[48,128]{1,0:T(8,128)S(1)}, u32[]{:S(2)}, u32[]{:S(2)}) collective-permute-start(f32[48,128]{1,0:T(8,128)S(1)} %get-tuple-element.18.after_ref.mine_ref), channel_id=1, source_target_pairs={{0,1},{1,2},{2,3},{3,4},{4,5},{5,6},{6,7},{7,8},{8,9},{9,10},{10,1... | collective-permute-start | bytes 73736 | tf_op jit(solution)/shard_map/ppermute | solution.py:344
  12.1 21.0 %collective-permute-start.3 = (f32[40,128]{1,0:T(8,128)S(1)}, f32[40,128]{1,0:T(8,128)S(1)}, u32[]{:S(2)}, u32[]{:S(2)}) collective-permute-start(f32[40,128]{1,0:T(8,128)S(1)} %get-tuple-element.25.after_ref), channel_id=1, source_target_pairs={{0,960},{64,0},{128,64},{192,128},{256,192},{320,256},{384,320},{4... | collective-permute-start | bytes 61448 | tf_op jit(solution)/shard_map/ppermute | solution.py:368
  30.0 5.7 %collective-permute-start.2 = (f32[40,128]{1,0:T(8,128)S(1)}, f32[40,128]{1,0:T(8,128)S(1)}, u32[]{:S(2)}, u32[]{:S(2)}) collective-permute-start(f32[40,128]{1,0:T(8,128)S(1)} %get-tuple-element.21.mine_ref), channel_id=1, source_target_pairs={{0,64},{64,128},{128,192},{192,256},{256,320},{320,384},{384,448},... | collective-permute-start | bytes 61448 | tf_op jit(solution)/shard_map/ppermute | solution.py:367
  37.8 36.5 %all-to-all-start = ((f32[16,1,19,512]{3,1,2,0:T(1,128)}), f32[16,1,19,512]{3,1,2,0:T(1,128)S(1)}, u32[]{:S(2)}, u32[]{:S(2)}) async-start(f32[16,1,19,512]{3,1,2,0:T(1,128)} %bitcast.3), calls=%async_computation | async-start | bytes 1245184 | tf_op jit(solution)/shard_map/all_to_all | solution.py:399

commit v3 on v2

--- a/solution.py
+++ b/solution.py
@@ -111,17 +111,21 @@
     return out
 
 
-def first_kernel(pdf_ref, grains_ref, moves_ref, col_ref, up_ref, dn_ref):
+def first_kernel(place_y_ref, pdf_ref, grains_ref, moves_ref, col_ref, near_ref, far_ref):
     lane = iota((ROWS, LANE), 1)
     col = collide([pdf_ref[q] for q in range(Q)])
     for q in range(Q):
         col_ref[q] = col[q]
-    for ref, chosen, edge in ((up_ref, YUP, LANE - Z), (dn_ref, YDN, 0)):
+    rims = []
+    for chosen, edge in ((YUP, LANE - Z), (YDN, 0)):
         rim = jnp.zeros((ROWS, LANE), F32)
         for k, q in enumerate(chosen):
             moved = pltpu.roll(z_shift(col[q], CZ[q], lane), (k * Z - edge) % LANE, 1)
             rim = jnp.where(lane // Z == k, moved, rim)
-        ref[0:ROWS, :] = rim
+        rims.append(rim)
+    left = place_y_ref[0] % 2 == 0
+    near_ref[0:ROWS, :] = jnp.where(left, rims[0], rims[1])
+    far_ref[0:ROWS, :] = jnp.where(left, rims[1], rims[0])
     moves = moves_ref[...]
     count = moves.shape[1]
     matches = (iota((16, count), 0) == moves).astype(F32)
@@ -134,7 +138,7 @@
     own = grains_ref[:, 0, :]
     high, middle, low = split3(own)
     packed = dot_nt(high, placing) + dot_nt(middle, placing) + dot_nt(low, placing)
-    for ref in (up_ref, dn_ref):
+    for ref in (near_ref, far_ref):
         ref[ROWS : ROWS + GV, :] = packed
         ref[ROWS + GV :, :] = jnp.zeros((6, LANE), F32)
 
@@ -154,28 +158,34 @@
     return plane
 
 
-def second_kernel(col_ref, mine_ref, ylo_ref, yhi_ref, after_ref, up_ref, dn_ref):
-    del after_ref
+def from_pairs(place_y_ref, near_ref, far_ref, start, size):
+    left = place_y_ref[0] % 2 == 0
+    low = slice(start, start + size)
+    high = slice(48 + start, 48 + start + size)
+    ylo = jnp.where(left, far_ref[low, :], near_ref[low, :])
+    yhi = jnp.where(left, near_ref[high, :], far_ref[high, :])
+    return ylo, yhi
+
+
+def second_kernel(place_y_ref, col_ref, mine_ref, near_ref, far_ref, up_ref, dn_ref):
     lane = iota((8, LANE), 1)
     for ref, chosen, part, row in ((up_ref, XUP, 8, 7), (dn_ref, XDN, 0, 0)):
         ref[0:8, :] = jnp.zeros((8, LANE), F32)
-        ylo = ylo_ref[part : part + 8, :]
-        yhi = yhi_ref[part : part + 8, :]
+        ylo, yhi = from_pairs(place_y_ref, near_ref, far_ref, part, 8)
         for k, q in enumerate(chosen):
             shifted = y_shifted(q, col_ref[q, part : part + 8, :], ylo, yhi, lane)
             ref[k : k + 1, :] = shifted[row : row + 1, :]
     grain_lane = iota((32, LANE), 1) // 8
+    ylo, yhi = from_pairs(place_y_ref, near_ref, far_ref, ROWS, 32)
     joined = jnp.where(
-        one_of(grain_lane, (2, 4, 7)),
-        ylo_ref[ROWS:, :],
-        jnp.where(one_of(grain_lane, (0, 3, 5)), yhi_ref[ROWS:, :], mine_ref[ROWS:, :]),
+        one_of(grain_lane, (2, 4, 7)), ylo, jnp.where(one_of(grain_lane, (0, 3, 5)), yhi, mine_ref[ROWS:, :])
     )
     up_ref[8:, :] = joined
     dn_ref[8:, :] = joined
 
 
-def link_kernel(place_x_ref, place_y_ref, link_ref, after_ref, kept_ref, arrived_ref, spread_ref, term_ref, dense_ref):
-    del after_ref
+def link_maps(place_x_ref, place_y_ref, link_ref, kept_parts, stay_parts, arrived_ref, spread_ref, term_ref, pick_ref):
+    toward = []
     for bx in range(2):
         cell = link_ref[0, bx : bx + 1, :]
         direction = link_ref[1, bx : bx + 1, :]
@@ -199,12 +209,16 @@
         terms += [jnp.where(direction <= 6, W6_AXIS, W6_DIAG), row.astype(F32)]
         for k, term in enumerate(terms):
             term_ref[bx, k : k + 1, :] = term
-        kept_ref[bx] = (iota((256, links), 0) == slot).astype(F32).astype(BF16)
-        arrived_ref[bx] = (iota((LANE, links), 0) + 256 == slot).astype(F32).astype(BF16)
+        kept = (iota((256, links), 0) == slot).astype(F32).astype(BF16)
+        arrived = (iota((LANE, links), 0) + 256 == slot).astype(F32).astype(BF16)
+        arrived_ref[bx] = arrived
+        picked = dot_nn(kept_parts, kept) + dot_nn(stay_parts, arrived)
+        pick_ref[bx] = picked[0:16] + picked[16:32] + picked[32:48]
         spread = (iota((LANE, links), 0) == side * 64 + cell % 64).astype(F32).astype(BF16)
         spread_ref[bx] = spread
         left = jnp.where(iota((8, links), 0) == row, direction.astype(F32), 0.0).astype(BF16)
-        dense_ref[8 * bx : 8 * bx + 8, :] = dot_nt(left, spread)
+        toward.append(dot_nt(left, spread))
+    return jnp.concatenate(toward, axis=0)
 
 
 def block_order(scratch_ref, plane):
@@ -217,14 +231,23 @@
     return first, second
 
 
-def shift_kernel(
-    col_ref, ylo_ref, yhi_ref, mine_ref, grains_ref, moves_ref, kept_ref, arrived_ref, dense_ref, after_ref,
-    plane_ref, value_ref, toward_ref, pick_ref, own_ref, scratch_ref,
+def prepare_kernel(
+    place_x_ref, place_y_ref, link_ref, col_ref, near_ref, far_ref, mine_ref, grains_ref, moves_ref, after_ref,
+    plane_ref, value_ref, toward_ref, pick_ref, own_ref, arrived_ref, spread_ref, term_ref, scratch_ref,
 ):
     del after_ref
     lane = iota((ROWS, LANE), 1)
-    ylo = ylo_ref[0:ROWS, :]
-    yhi = yhi_ref[0:ROWS, :]
+    kept = jnp.where(moves_ref[...] == 4, grains_ref[:, 0, :], 0.0)
+    own_ref[...] = kept
+    stay = jnp.where(one_of(iota((16, LANE), 1) // 8, (3, 4)), mine_ref[8:24, :], 0.0)
+    kept_parts = jnp.concatenate(split3(kept[0:16]), axis=0)
+    stay_parts = jnp.concatenate(split3(stay), axis=0)
+    toward = link_maps(
+        place_x_ref, place_y_ref, link_ref, kept_parts, stay_parts, arrived_ref, spread_ref, term_ref, pick_ref
+    )
+    for half, part in enumerate(block_order(scratch_ref.at[0], toward)):
+        toward_ref[half] = part.astype(I32)
+    ylo, yhi = from_pairs(place_y_ref, near_ref, far_ref, 0, ROWS)
     for q in range(Q):
         plane = y_shifted(q, col_ref[q], ylo, yhi, lane)
         if CX[q]:
@@ -232,17 +255,6 @@
         for ref, given in ((plane_ref, plane), (value_ref, col_ref[OPP[q]])):
             for half, part in enumerate(block_order(scratch_ref.at[q % 4 + (4 if ref is value_ref else 0)], given)):
                 ref[q, half] = part
-    for half, part in enumerate(block_order(scratch_ref.at[0], dense_ref[...])):
-        toward_ref[half] = part.astype(I32)
-    kept = jnp.where(moves_ref[...] == 4, grains_ref[:, 0, :], 0.0)
-    own_ref[...] = kept
-    stay = one_of(iota((32, LANE), 1) // 8, (3, 4))
-    arrived = jnp.where(stay, mine_ref[8:, :], 0.0)
-    kept_parts = jnp.concatenate(split3(kept[0:16]), axis=0)
-    arrived_parts = jnp.concatenate(split3(arrived[0:16]), axis=0)
-    for bx in range(2):
-        picked = dot_nn(kept_parts, kept_ref[bx]) + dot_nn(arrived_parts, arrived_ref[bx])
-        pick_ref[bx] = picked[0:16] + picked[16:32] + picked[32:48]
 
 
 def table_kernel(mine_ref, xlo_ref, xhi_ref, own_ref, table_ref):
@@ -321,6 +333,12 @@
     return [(i, (i + step) % count) for i in range(count)]
 
 
+def pair_gather(message, axis, first):
+    count = lax.axis_size(axis)
+    groups = [[i, (i + 1) % count] for i in range(first, count, 2)]
+    return lax.all_gather(message, axis, axis=0, tiled=True, axis_index_groups=groups)
+
+
 def near(*arrays):
     return tuple(pltpu.with_memory_space_constraint(a, pltpu.VMEM) for a in arrays)
 
@@ -334,53 +352,43 @@
     place_x = lax.axis_index("gx").astype(I32).reshape(1)
     place_y = lax.axis_index("gy").astype(I32).reshape(1)
     links = link_lists.shape[2]
-    col, y_up, y_dn = pl.pallas_call(
+    col, near_msg, far_msg = pl.pallas_call(
         first_kernel,
         out_shape=(chip(Q, ROWS, LANE), chip(48, LANE), chip(48, LANE)),
-        in_specs=[VMEM] * 3,
+        in_specs=[SMEM] + [VMEM] * 3,
         out_specs=(VMEM,) * 3,
         name="collide_pack",
-    )(pdf, grains, grain_moves)
-    ylo = lax.ppermute(y_up, "gy", ring("gy", 1))
-    yhi = lax.ppermute(y_dn, "gy", ring("gy", -1))
-    kept, arrived, spread, terms, dense = pl.pallas_call(
-        link_kernel,
-        out_shape=(
-            chip(2, 256, links, dtype=BF16),
-            chip(2, LANE, links, dtype=BF16),
-            chip(2, LANE, links, dtype=BF16),
-            chip(2, 8, links),
-            chip(ROWS, LANE),
-        ),
-        in_specs=[SMEM, SMEM, VMEM, VMEM],
-        out_specs=(VMEM,) * 5,
-        cost_estimate=pl.CostEstimate(flops=4_000_000, bytes_accessed=1_000_000, transcendentals=0),
-        name="link_maps",
-    )(place_x, place_y, link_lists, *near(y_up))
+    )(place_y, pdf, grains, grain_moves)
+    near_pair = pair_gather(near_msg, "gy", 0)
+    near_pair, far_msg = lax.optimization_barrier((near_pair, far_msg))
+    far_pair = pair_gather(far_msg, "gy", 1)
     x_up, x_dn = pl.pallas_call(
         second_kernel,
         out_shape=(chip(40, LANE), chip(40, LANE)),
-        in_specs=[VMEM] * 5,
+        in_specs=[SMEM] + [VMEM] * 4,
         out_specs=(VMEM,) * 2,
         name="x_messages",
-    )(*near(col, y_up, ylo, yhi, terms))
+    )(place_y, *near(col, near_msg, near_pair, far_pair))
     xlo = lax.ppermute(x_up, "gx", ring("gx", 1))
     xhi = lax.ppermute(x_dn, "gx", ring("gx", -1))
-    plane, value, toward, pick, own = pl.pallas_call(
-        shift_kernel,
+    plane, value, toward, pick, own, arrived, spread, terms = pl.pallas_call(
+        prepare_kernel,
         out_shape=(
             chip(Q, 2, 8, LANE),
             chip(Q, 2, 8, LANE),
             chip(2, 8, LANE, dtype=I32),
             chip(2, 16, links),
             chip(GV, 256),
+            chip(2, LANE, links, dtype=BF16),
+            chip(2, LANE, links, dtype=BF16),
+            chip(2, 8, links),
         ),
-        in_specs=[VMEM] * 10,
-        out_specs=(VMEM,) * 5,
+        in_specs=[SMEM, SMEM] + [VMEM] * 8,
+        out_specs=(VMEM,) * 8,
         scratch_shapes=[pltpu.VMEM((8, ROWS, LANE), F32)],
         cost_estimate=pl.CostEstimate(flops=4_000_000, bytes_accessed=1_000_000, transcendentals=0),
-        name="shift_planes",
-    )(*near(col, ylo, yhi, x_up), grains, grain_moves, *near(kept, arrived, dense, x_dn))
+        name="prepare",
+    )(place_x, place_y, link_lists, *near(col, near_pair, far_pair, x_up), grains, grain_moves, *near(x_dn))
     send = pl.pallas_call(
         finish_kernel,
         out_shape=jax.ShapeDtypeStruct((group * Q, 4, LANE), F32),

time: 75.6 us -> 74.1 us (0.980)
  blocking collectives: 0 us -> 9.41 us
  starting transfers between devices: 32.3 us -> 23.5 us
  waiting for transfers between devices: 35 us -> 34 us
  Pallas kernels: 6.32 us -> 5.4 us
    all_gather x0 -> x2, blocking collectives: none -> 9.41 us  [pair_gather(): lax.all_gather(message, axis, axis=0, tiled=True, axis_index_groups=groups)]
    ppermute x2 -> x0, starting transfers between devices: 8.88 us -> none  [the longest x1 6.3 us: body(): ylo = lax.ppermute(y_up, 'gy', ring('gy', 1))]
    pallas_call x2 -> x1, Pallas kernels: 2.23 us -> 1.31 us  [body(): pl.pallas_call(prepare_kernel, out_shape=(chip(Q, 2, 8, LANE), chip(Q, 2,...]
    all_to_all x1, waiting for transfers between devices: 32.3 us -> 31.5 us  [body(): lax.all_to_all(send.reshape(group, 1, Q, 512), 'gx', split_axis=0, concat...]
  transfers between devices with their start and end apart: 5 -> 3, of which waited for: 2 -> 2; matrix products, arithmetic and copies ran while one was open for 0% -> 0% of each run, Pallas kernels for 4% -> 3%
where the time goes in v3:
time: 74.1 us; the launch traced here: 73.7 us
  waiting for transfers between devices  34 us (46%)
  starting transfers between devices  23.5 us (32%)
  blocking collectives  9.41 us (13%)
  Pallas kernels  5.4 us (7%)
  local copies, waits for them, and re-layouts  0.83 us (1%)
    all_to_all x1, waiting for transfers between devices, body(): lax.all_to_all(send.reshape(group, 1, Q, 512), 'gx', split_axis=0, concat...  31.5 us
    ppermute x1, starting transfers between devices, body(): xhi = lax.ppermute(x_dn, 'gx', ring('gx', -1))  17.9 us
    all_gather x2, blocking collectives, pair_gather(): lax.all_gather(message, axis, axis=0, tiled=True, axis_index_groups=groups)  9.41 us
    all_to_all x1, starting transfers between devices, body(): lax.all_to_all(send.reshape(group, 1, Q, 512), 'gx', split_axis=0, concat...  3.59 us
    ppermute x1, waiting for transfers between devices, body(): xlo = lax.ppermute(x_up, 'gx', ring('gx', 1))  2.49 us
    pallas_call x1, Pallas kernels, body(): pl.pallas_call(finish_kernel, out_shape=jax.ShapeDtypeStruct((group * Q,...  2.02 us
    ppermute x1, starting transfers between devices, body(): xlo = lax.ppermute(x_up, 'gx', ring('gx', 1))  1.92 us
  transfers between devices with their start and end apart: 3, of which 2 were waited for; matrix products, arithmetic and copies ran while one was open for 0% of the time, Pallas kernels for 3%

profile of v3, /device:TPU:31, one launch (start us, length us, event | category | flops | bytes accessed | tf_op | source)
XLA Modules:
  0.0 73.7 jit_solution(9307604336670419609)
XLA Ops:
  0.6 1.3 %collide_pack.1 = (f32[19,16,128]{2,1,0:T(8,128)S(1)}, f32[48,128]{1,0:T(8,128)S(1)}, f32[48,128]{1,0:T(8,128)S(1)}) custom-call(s32[1]{0:T(128)} %bitcast.1.place_y_ref, f32[19,16,128]{2,1,0:T(8,128)} %pdf_ref.1, f32[26,1,256]{2,1,0:T(1,128)} %grains_ref.3, s32[1,256]{1,0:T(1,128)} %moves_ref.3), custom_call_target="tpu_custom_call" | custom-call | tf_op jit(solution)/shard_map/collide_pack/pallas_call | solution.py:355
  2.0 2.2 %all_gather.6.near_ref = f32[96,128]{1,0:T(8,128)S(1)} all-gather(f32[48,128]{1,0:T(8,128)S(1)} %get-tuple-element.18.mine_ref), channel_id=1, replica_groups={{0,1},{2,3},{4,5},{6,7},{8,9},{10,11},{12,13},{14,15},{16,17},{18,19},{..., dimensions={0}, use_global_device_ids=true | all-gather | bytes 73728 | tf_op jit(solution)/shard_map/all_gather | solution.py:339
  4.1 7.2 %all_gather.7.far_ref = f32[96,128]{1,0:T(8,128)S(1)} all-gather(f32[48,128]{1,0:T(8,128)S(1)} %get-tuple-element.21), channel_id=1, replica_groups={{1,2},{3,4},{5,6},{7,8},{9,10},{11,12},{13,14},{15,16},{17,18},{19,20},..., dimensions={0}, use_global_device_ids=true | all-gather | bytes 73728 | tf_op jit(solution)/shard_map/all_gather | solution.py:339
  11.4 0.1 x_messages.1
  11.5 17.9 %collective-permute-start.1 = (f32[40,128]{1,0:T(8,128)S(1)}, f32[40,128]{1,0:T(8,128)S(1)}, u32[]{:S(2)}, u32[]{:S(2)}) collective-permute-start(f32[40,128]{1,0:T(8,128)S(1)} %get-tuple-element.23.after_ref), channel_id=1, source_target_pairs={{0,960},{64,0},{128,64},{192,128},{256,192},{320,256},{384,320},{4... | collective-permute-start | bytes 61448 | tf_op jit(solution)/shard_map/ppermute | solution.py:373
  29.4 1.9 %collective-permute-start = (f32[40,128]{1,0:T(8,128)S(1)}, f32[40,128]{1,0:T(8,128)S(1)}, u32[]{:S(2)}, u32[]{:S(2)}) collective-permute-start(f32[40,128]{1,0:T(8,128)S(1)} %get-tuple-element.22.mine_ref), channel_id=1, source_target_pairs={{0,64},{64,128},{128,192},{192,256},{256,320},{320,384},{384,448},... | collective-permute-start | bytes 61448 | tf_op jit(solution)/shard_map/ppermute | solution.py:372
  31.4 1.3 %prepare.1 = (f32[19,2,8,128]{3,2,1,0:T(8,128)S(1)}, f32[19,2,8,128]{3,2,1,0:T(8,128)S(1)}, s32[2,8,128]{2,1,0:T(8,128)S(1)}, f32[2,16,512]{2,1,0:T(8,128)S(1)},...) custom-call(s32[1]{0:T(128)} %bitcast.place_x_ref, ...), custom_call_target="tpu_custom_call" | custom-call | flops 4000000 | bytes 1000000 | tf_op jit(solution)/shard_map/prepare/pallas_call | solution.py:374
  32.7 0.0 collective-permute-done.1.xhi_ref
  32.7 2.5 %collective-permute-done.xlo_ref = f32[40,128]{1,0:T(8,128)S(1)} collective-permute-done((f32[40,128]{1,0:T(8,128)S(1)}, f32[40,128]{1,0:T(8,128)S(1)}, u32[]{:S(2)}, u32[]{:S(2)}) %collective-permute-start) | collective-permute-done | bytes 20512 | tf_op jit(solution)/shard_map/ppermute | solution.py:372
  35.2 2.0 %finish_blocks.1 = f32[304,4,128]{2,1,0:T(4,128)} custom-call(s32[2,2]{1,0:T(2,128)} %owner_ref.1, f32[19,2,8,128]{3,2,1,0:T(8,128)S(1)} %get-tuple-element.24.plane_ref, f32[19,2,8,128]{3,2,1,0:T(8,128)S(1)} %get-tuple-element.25.value_ref, s32[2,8,128]{2,1,0:T(8,128)S(1)} %get-tuple-element.26.toward_ref, f32[40,128]{1,0:T(8,128)S(1)} %collective-permute-done.xlo_ref, ...), custom_call_target="tpu_custom_call" | custom-call | tf_op jit(solution)/shard_map/finish_blocks/pallas_call | solution.py:392
  37.2 3.6 %all-to-all-start = ((f32[16,1,19,512]{3,1,2,0:T(1,128)}), f32[16,1,19,512]{3,1,2,0:T(1,128)S(1)}, u32[]{:S(2)}, u32[]{:S(2)}) async-start(f32[16,1,19,512]{3,1,2,0:T(1,128)} %bitcast.3), calls=%async_computation | async-start | bytes 1245184 | tf_op jit(solution)/shard_map/all_to_all | solution.py:407
  40.8 0.6 grain_table.1
  41.4 31.5 %all-to-all-done = f32[16,1,19,512]{3,1,2,0:T(1,128)S(1)} async-done(((f32[16,1,19,512]{3,1,2,0:T(1,128)}), f32[16,1,19,512]{3,1,2,0:T(1,128)S(1)}, u32[]{:S(2)}, u32[]{:S(2)}) %all-to-all-start) | async-done | bytes 622624 | tf_op jit(solution)/shard_map/all_to_all | solution.py:407
  72.9 0.8 %copy.11 = f32[16,1,19,512]{3,1,2,0:T(1,128)} copy(f32[16,1,19,512]{3,1,2,0:T(1,128)S(1)} %all-to-all-done) | data formatting | bytes 1245184
Async XLA Ops:
  11.5 21.2 %collective-permute-start.1 = (f32[40,128]{1,0:T(8,128)S(1)}, f32[40,128]{1,0:T(8,128)S(1)}, u32[]{:S(2)}, u32[]{:S(2)}) collective-permute-start(f32[40,128]{1,0:T(8,128)S(1)} %get-tuple-element.23.after_ref), channel_id=1, source_target_pairs={{0,960},{64,0},{128,64},{192,128},{256,192},{320,256},{384,320},{4... | collective-permute-start | bytes 61448 | tf_op jit(solution)/shard_map/ppermute | solution.py:373
  29.4 5.7 %collective-permute-start = (f32[40,128]{1,0:T(8,128)S(1)}, f32[40,128]{1,0:T(8,128)S(1)}, u32[]{:S(2)}, u32[]{:S(2)}) collective-permute-start(f32[40,128]{1,0:T(8,128)S(1)} %get-tuple-element.22.mine_ref), channel_id=1, source_target_pairs={{0,64},{64,128},{128,192},{192,256},{256,320},{320,384},{384,448},... | collective-permute-start | bytes 61448 | tf_op jit(solution)/shard_map/ppermute | solution.py:372
  37.2 35.7 %all-to-all-start = ((f32[16,1,19,512]{3,1,2,0:T(1,128)}), f32[16,1,19,512]{3,1,2,0:T(1,128)S(1)}, u32[]{:S(2)}, u32[]{:S(2)}) async-start(f32[16,1,19,512]{3,1,2,0:T(1,128)} %bitcast.3), calls=%async_computation | async-start | bytes 1245184 | tf_op jit(solution)/shard_map/all_to_all | solution.py:407

commit v4 on v3

--- a/solution.py
+++ b/solution.py
@@ -162,8 +162,9 @@
     left = place_y_ref[0] % 2 == 0
     low = slice(start, start + size)
     high = slice(48 + start, 48 + start + size)
-    ylo = jnp.where(left, far_ref[low, :], near_ref[low, :])
-    yhi = jnp.where(left, near_ref[high, :], far_ref[high, :])
+    far = far_ref[low, :]
+    ylo = jnp.where(left, far, near_ref[low, :])
+    yhi = jnp.where(left, near_ref[high, :], far)
     return ylo, yhi
 
 
@@ -269,10 +270,10 @@
 
 
 def finish_kernel(
-    owner_ref, plane_ref, value_ref, toward_ref, xlo_ref, xhi_ref, pick_ref,
-    arrived_ref, spread_ref, term_ref, send_ref, scratch_ref,
+    owner_ref, empty_ref, plane_ref, value_ref, toward_ref, xlo_ref, xhi_ref, pick_ref,
+    arrived_ref, spread_ref, term_ref, send_ref, scratch_ref, block_ref, sems,
 ):
-    send_ref[...] = jnp.zeros(send_ref.shape, F32)
+    del empty_ref
     grain_lane = iota((16, LANE), 1) // 8
     moved = jnp.where(
         one_of(grain_lane, (5, 6, 7)),
@@ -300,7 +301,6 @@
         corrections.append(dense[0:8] + dense[8:16] + dense[16:24])
     correction = jnp.concatenate(corrections, axis=0)
     correction = block_order(scratch_ref, correction)
-    base = [owner_ref[n // 2, n % 2] * Q for n in range(4)]
     low_half = iota((8, LANE), 1) < 64
     row = iota((8, LANE), 0)
     first_row = jnp.logical_and(row == 0, low_half)
@@ -320,8 +320,21 @@
                 part = jnp.where(last_row, edge, part)
             if q:
                 part = jnp.where(toward_ref[half] == OPP[q], value_ref[q, half] - correction[half], part)
-            send_ref[base[half] + q] = part[0:4]
-            send_ref[base[2 + half] + q] = part[4:8]
+            block_ref[half, q] = part[0:4]
+            block_ref[2 + half, q] = part[4:8]
+    stores = [
+        pltpu.make_async_copy(block_ref.at[n], send_ref.at[pl.ds(owner_ref[n // 2, n % 2] * Q, Q)], sems.at[n])
+        for n in range(4)
+    ]
+    for copy in stores:
+        copy.start()
+    for copy in stores:
+        copy.wait()
+
+
+def clear_kernel(after_ref, send_ref):
+    del after_ref
+    send_ref[...] = jnp.zeros(send_ref.shape, F32)
 
 
 VMEM = pl.BlockSpec(memory_space=pltpu.VMEM)
@@ -331,12 +344,6 @@
 def ring(axis, step):
     count = lax.axis_size(axis)
     return [(i, (i + step) % count) for i in range(count)]
-
-
-def pair_gather(message, axis, first):
-    count = lax.axis_size(axis)
-    groups = [[i, (i + 1) % count] for i in range(first, count, 2)]
-    return lax.all_gather(message, axis, axis=0, tiled=True, axis_index_groups=groups)
 
 
 def near(*arrays):
@@ -359,9 +366,11 @@
         out_specs=(VMEM,) * 3,
         name="collide_pack",
     )(place_y, pdf, grains, grain_moves)
-    near_pair = pair_gather(near_msg, "gy", 0)
-    near_pair, far_msg = lax.optimization_barrier((near_pair, far_msg))
-    far_pair = pair_gather(far_msg, "gy", 1)
+    columns = lax.axis_size("gy")
+    far_pair = lax.ppermute(far_msg, "gy", [(i, (i + 2 * (i % 2) - 1) % columns) for i in range(columns)])
+    near_pair = lax.all_gather(
+        near_msg, "gy", axis=0, tiled=True, axis_index_groups=[[i, i + 1] for i in range(0, columns, 2)]
+    )
     x_up, x_dn = pl.pallas_call(
         second_kernel,
         out_shape=(chip(40, LANE), chip(40, LANE)),
@@ -389,14 +398,27 @@
         cost_estimate=pl.CostEstimate(flops=4_000_000, bytes_accessed=1_000_000, transcendentals=0),
         name="prepare",
     )(place_x, place_y, link_lists, *near(col, near_pair, far_pair, x_up), grains, grain_moves, *near(x_dn))
+    empty = pl.pallas_call(
+        clear_kernel,
+        out_shape=jax.ShapeDtypeStruct((group * Q, 4, LANE), F32),
+        in_specs=[VMEM],
+        out_specs=VMEM,
+        cost_estimate=pl.CostEstimate(flops=4_000_000, bytes_accessed=1_000_000, transcendentals=0),
+        name="clear_slots",
+    )(*near(x_dn))
     send = pl.pallas_call(
         finish_kernel,
         out_shape=jax.ShapeDtypeStruct((group * Q, 4, LANE), F32),
-        in_specs=[SMEM] + [VMEM] * 9,
-        out_specs=VMEM,
-        scratch_shapes=[pltpu.VMEM((ROWS, LANE), F32)],
+        in_specs=[SMEM, pl.BlockSpec(memory_space=pl.ANY)] + [VMEM] * 9,
+        out_specs=pl.BlockSpec(memory_space=pl.ANY),
+        input_output_aliases={1: 0},
+        scratch_shapes=[
+            pltpu.VMEM((ROWS, LANE), F32),
+            pltpu.VMEM((4, Q, 4, LANE), F32),
+            pltpu.SemaphoreType.DMA((4,)),
+        ],
         name="finish_blocks",
-    )(owner_map, *near(plane, value, toward, xlo, xhi, pick, arrived, spread, terms))
+    )(owner_map, empty, *near(plane, value, toward, xlo, xhi, pick, arrived, spread, terms))
     table = pl.pallas_call(
         table_kernel,
         out_shape=jax.ShapeDtypeStruct((GV, 1, 320), F32),

time: 74.1 us -> 74 us (level)
  the two profiles are of different devices: /device:TPU:31 before, /device:TPU:64 now
where the time goes in v4:
time: 74 us; the launch traced here: 73.6 us
  waiting for transfers between devices  34.7 us (47%)
  starting transfers between devices  29.4 us (40%)
  Pallas kernels  6.12 us (8%)
  blocking collectives  1.84 us (2%)
  local copies, waits for them, and re-layouts  0.83 us (1%)
    all_to_all x1, waiting for transfers between devices, body(): lax.all_to_all(send.reshape(group, 1, Q, 512), 'gx', split_axis=0, concat...  31.2 us
    ppermute x1, starting transfers between devices, body(): xhi = lax.ppermute(x_dn, 'gx', ring('gx', -1))  13.8 us
    ppermute x1, starting transfers between devices, body(): lax.ppermute(far_msg, 'gy', [(i, (i + 2 * (i % 2) - 1) % columns) for i i...  7.01 us
    all_to_all x1, starting transfers between devices, body(): lax.all_to_all(send.reshape(group, 1, Q, 512), 'gx', split_axis=0, concat...  6.62 us
    ppermute x1, waiting for transfers between devices, body(): xlo = lax.ppermute(x_up, 'gx', ring('gx', 1))  3.58 us
    ppermute x1, starting transfers between devices, body(): xlo = lax.ppermute(x_up, 'gx', ring('gx', 1))  1.92 us
    pallas_call x1, Pallas kernels, body(): pl.pallas_call(finish_kernel, out_shape=jax.ShapeDtypeStruct((group * Q,...  1.85 us
    all_gather x1, blocking collectives, body(): lax.all_gather(near_msg, 'gy', axis=0, tiled=True, axis_index_groups=[[i,...  1.84 us
  transfers between devices with their start and end apart: 4, of which 2 were waited for; matrix products, arithmetic and copies ran while one was open for 0% of the time, Pallas kernels for 4%

profile of v4, /device:TPU:64, one launch (start us, length us, event | category | flops | bytes accessed | tf_op | source)
XLA Modules:
  0.0 73.6 jit_solution(18132790197521633419)
XLA Ops:
  0.6 1.3 %collide_pack.1 = (f32[19,16,128]{2,1,0:T(8,128)S(1)}, f32[48,128]{1,0:T(8,128)S(1)}, f32[48,128]{1,0:T(8,128)S(1)}) custom-call(s32[1]{0:T(128)} %bitcast.place_y_ref, f32[19,16,128]{2,1,0:T(8,128)} %pdf_ref.1, f32[26,1,256]{2,1,0:T(1,128)} %grains_ref.3, s32[1,256]{1,0:T(1,128)} %moves_ref.3), custom_call_target="tpu_custom_call" | custom-call | tf_op jit(solution)/shard_map/collide_pack/pallas_call | solution.py:362
  2.0 7.0 %collective-permute-start = (f32[48,128]{1,0:T(8,128)S(1)}, f32[48,128]{1,0:T(8,128)S(1)}, u32[]{:S(2)}, u32[]{:S(2)}) collective-permute-start(f32[48,128]{1,0:T(8,128)S(1)} %get-tuple-element.17), channel_id=1, source_target_pairs={{0,63},{1,2},{2,1},{3,4},{4,3},{5,6},{6,5},{7,8},{8,7},{9,10},{10,... | collective-permute-start | bytes 73736 | tf_op jit(solution)/shard_map/ppermute | solution.py:370
  9.0 1.8 %all_gather.3.near_ref = f32[96,128]{1,0:T(8,128)S(1)} all-gather(f32[48,128]{1,0:T(8,128)S(1)} %get-tuple-element.16.mine_ref), channel_id=1, replica_groups={{0,1},{2,3},{4,5},{6,7},{8,9},{10,11},{12,13},{14,15},{16,17},{18,19},{..., dimensions={0}, use_global_device_ids=true | all-gather | bytes 73728 | tf_op jit(solution)/shard_map/all_gather | solution.py:371
  10.8 0.0 collective-permute-done.far_ref
  10.8 0.1 x_messages.1
  10.9 13.8 %collective-permute-start.2 = (f32[40,128]{1,0:T(8,128)S(1)}, f32[40,128]{1,0:T(8,128)S(1)}, u32[]{:S(2)}, u32[]{:S(2)}) collective-permute-start(f32[40,128]{1,0:T(8,128)S(1)} %get-tuple-element.18.after_ref), channel_id=1, source_target_pairs={{0,960},{64,0},{128,64},{192,128},{256,192},{320,256},{384,320},{4... | collective-permute-start | bytes 61448 | tf_op jit(solution)/shard_map/ppermute | solution.py:382
  24.7 1.9 %collective-permute-start.1 = (f32[40,128]{1,0:T(8,128)S(1)}, f32[40,128]{1,0:T(8,128)S(1)}, u32[]{:S(2)}, u32[]{:S(2)}) collective-permute-start(f32[40,128]{1,0:T(8,128)S(1)} %get-tuple-element.19.mine_ref), channel_id=1, source_target_pairs={{0,64},{64,128},{128,192},{192,256},{256,320},{320,384},{384,448},... | collective-permute-start | bytes 61448 | tf_op jit(solution)/shard_map/ppermute | solution.py:381
  26.7 0.9 %clear_slots.1.empty_ref = f32[304,4,128]{2,1,0:T(4,128)} custom-call(f32[40,128]{1,0:T(8,128)S(1)} %get-tuple-element.18.after_ref), custom_call_target="tpu_custom_call" | custom-call | flops 4000000 | bytes 1000000 | tf_op jit(solution)/shard_map/clear_slots/pallas_call | solution.py:401
  27.6 1.3 %prepare.1 = (f32[19,2,8,128]{3,2,1,0:T(8,128)S(1)}, f32[19,2,8,128]{3,2,1,0:T(8,128)S(1)}, s32[2,8,128]{2,1,0:T(8,128)S(1)}, f32[2,16,512]{2,1,0:T(8,128)S(1)},...) custom-call(s32[1]{0:T(128)} %bitcast.1.place_x_ref, ...), custom_call_target="tpu_custom_call" | custom-call | flops 4000000 | bytes 1000000 | tf_op jit(solution)/shard_map/prepare/pallas_call | solution.py:383
  28.9 0.0 collective-permute-done.2.xhi_ref
  28.9 3.6 %collective-permute-done.1.xlo_ref = f32[40,128]{1,0:T(8,128)S(1)} collective-permute-done((f32[40,128]{1,0:T(8,128)S(1)}, f32[40,128]{1,0:T(8,128)S(1)}, u32[]{:S(2)}, u32[]{:S(2)}) %collective-permute-start.1) | collective-permute-done | bytes 20512 | tf_op jit(solution)/shard_map/ppermute | solution.py:381
  32.5 1.9 %finish_blocks.1 = f32[304,4,128]{2,1,0:T(4,128)} custom-call(s32[2,2]{1,0:T(2,128)} %owner_ref.1, f32[304,4,128]{2,1,0:T(4,128)} %clear_slots.1.empty_ref, f32[19,2,8,128]{3,2,1,0:T(8,128)S(1)} %get-tuple-element.20.plane_ref, f32[19,2,8,128]{3,2,1,0:T(8,128)S(1)} %get-tuple-element.21.value_ref, ...), custom_call_target="tpu_custom_call", output_to_operand_aliasing={{}: (1, {})} | custom-call | tf_op jit(solution)/shard_map/finish_blocks/pallas_call | solution.py:409
  34.3 6.6 %all-to-all-start = ((f32[16,1,19,512]{3,1,2,0:T(1,128)}), f32[16,1,19,512]{3,1,2,0:T(1,128)S(1)}, u32[]{:S(2)}, u32[]{:S(2)}) async-start(f32[16,1,19,512]{3,1,2,0:T(1,128)} %bitcast.3), calls=%async_computation | async-start | bytes 1245184 | tf_op jit(solution)/shard_map/all_to_all | solution.py:429
  40.9 0.6 grain_table.1
  41.6 31.2 %all-to-all-done = f32[16,1,19,512]{3,1,2,0:T(1,128)S(1)} async-done(((f32[16,1,19,512]{3,1,2,0:T(1,128)}), f32[16,1,19,512]{3,1,2,0:T(1,128)S(1)}, u32[]{:S(2)}, u32[]{:S(2)}) %all-to-all-start) | async-done | bytes 622624 | tf_op jit(solution)/shard_map/all_to_all | solution.py:429
  72.7 0.8 %copy.13 = f32[16,1,19,512]{3,1,2,0:T(1,128)} copy(f32[16,1,19,512]{3,1,2,0:T(1,128)S(1)} %all-to-all-done) | data formatting | bytes 1245184
Async XLA Ops:
  2.0 8.9 %collective-permute-start = (f32[48,128]{1,0:T(8,128)S(1)}, f32[48,128]{1,0:T(8,128)S(1)}, u32[]{:S(2)}, u32[]{:S(2)}) collective-permute-start(f32[48,128]{1,0:T(8,128)S(1)} %get-tuple-element.17), channel_id=1, source_target_pairs={{0,63},{1,2},{2,1},{3,4},{4,3},{5,6},{6,5},{7,8},{8,7},{9,10},{10,... | collective-permute-start | bytes 73736 | tf_op jit(solution)/shard_map/ppermute | solution.py:370
  10.9 18.0 %collective-permute-start.2 = (f32[40,128]{1,0:T(8,128)S(1)}, f32[40,128]{1,0:T(8,128)S(1)}, u32[]{:S(2)}, u32[]{:S(2)}) collective-permute-start(f32[40,128]{1,0:T(8,128)S(1)} %get-tuple-element.18.after_ref), channel_id=1, source_target_pairs={{0,960},{64,0},{128,64},{192,128},{256,192},{320,256},{384,320},{4... | collective-permute-start | bytes 61448 | tf_op jit(solution)/shard_map/ppermute | solution.py:382
  24.7 7.7 %collective-permute-start.1 = (f32[40,128]{1,0:T(8,128)S(1)}, f32[40,128]{1,0:T(8,128)S(1)}, u32[]{:S(2)}, u32[]{:S(2)}) collective-permute-start(f32[40,128]{1,0:T(8,128)S(1)} %get-tuple-element.19.mine_ref), channel_id=1, source_target_pairs={{0,64},{64,128},{128,192},{192,256},{256,320},{320,384},{384,448},... | collective-permute-start | bytes 61448 | tf_op jit(solution)/shard_map/ppermute | solution.py:381
  34.3 38.4 %all-to-all-start = ((f32[16,1,19,512]{3,1,2,0:T(1,128)}), f32[16,1,19,512]{3,1,2,0:T(1,128)S(1)}, u32[]{:S(2)}, u32[]{:S(2)}) async-start(f32[16,1,19,512]{3,1,2,0:T(1,128)} %bitcast.3), calls=%async_computation | async-start | bytes 1245184 | tf_op jit(solution)/shard_map/all_to_all | solution.py:429

commit v5 on v4

--- a/solution.py
+++ b/solution.py
@@ -168,21 +168,33 @@
     return ylo, yhi
 
 
-def second_kernel(place_y_ref, col_ref, mine_ref, near_ref, far_ref, up_ref, dn_ref):
+def second_kernel(place_x_ref, place_y_ref, col_ref, mine_ref, near_ref, far_ref, first_ref, other_ref):
+    even = place_x_ref[0] % 2 == 0
     lane = iota((8, LANE), 1)
-    for ref, chosen, part, row in ((up_ref, XUP, 8, 7), (dn_ref, XDN, 0, 0)):
-        ref[0:8, :] = jnp.zeros((8, LANE), F32)
+    rims = []
+    for chosen, part, row in ((XUP, 8, 7), (XDN, 0, 0)):
         ylo, yhi = from_pairs(place_y_ref, near_ref, far_ref, part, 8)
-        for k, q in enumerate(chosen):
+        lines = []
+        for q in chosen:
             shifted = y_shifted(q, col_ref[q, part : part + 8, :], ylo, yhi, lane)
-            ref[k : k + 1, :] = shifted[row : row + 1, :]
+            lines.append(shifted[row : row + 1, :])
+        rims.append(jnp.concatenate(lines + [jnp.zeros((3, LANE), F32)], axis=0))
+    first_ref[0:8, :] = jnp.where(even, rims[0], rims[1])
+    other_ref[0:8, :] = jnp.where(even, rims[1], rims[0])
     grain_lane = iota((32, LANE), 1) // 8
     ylo, yhi = from_pairs(place_y_ref, near_ref, far_ref, ROWS, 32)
     joined = jnp.where(
         one_of(grain_lane, (2, 4, 7)), ylo, jnp.where(one_of(grain_lane, (0, 3, 5)), yhi, mine_ref[ROWS:, :])
     )
-    up_ref[8:, :] = joined
-    dn_ref[8:, :] = joined
+    first_ref[8:, :] = joined
+    other_ref[8:, :] = joined
+
+
+def from_rows(place_x_ref, first_ref, other_ref, start, size):
+    even = place_x_ref[0] % 2 == 0
+    first = first_ref[start : start + size, :]
+    other = other_ref[start : start + size, :]
+    return jnp.where(even, other, first), jnp.where(even, first, other)
 
 
 def link_maps(place_x_ref, place_y_ref, link_ref, kept_parts, stay_parts, arrived_ref, spread_ref, term_ref, pick_ref):
@@ -258,28 +270,26 @@
                 ref[q, half] = part
 
 
-def table_kernel(mine_ref, xlo_ref, xhi_ref, own_ref, table_ref):
+def table_kernel(place_x_ref, mine_ref, first_ref, other_ref, own_ref, table_ref):
+    xlo, xhi = from_rows(place_x_ref, first_ref, other_ref, 8, 32)
     grain_lane = iota((32, LANE), 1) // 8
     arrived = jnp.where(
         one_of(grain_lane, (5, 6, 7)),
-        xlo_ref[8:, :],
-        jnp.where(one_of(grain_lane, (0, 1, 2)), xhi_ref[8:, :], mine_ref[8:, :]),
+        xlo,
+        jnp.where(one_of(grain_lane, (0, 1, 2)), xhi, mine_ref[8:, :]),
     )
     table_ref[:, 0, 0:256] = own_ref[...]
     table_ref[:, 0, 256:320] = arrived[0:GV, 0:64]
 
 
 def finish_kernel(
-    owner_ref, empty_ref, plane_ref, value_ref, toward_ref, xlo_ref, xhi_ref, pick_ref,
+    owner_ref, place_x_ref, empty_ref, plane_ref, value_ref, toward_ref, first_ref, other_ref, pick_ref,
     arrived_ref, spread_ref, term_ref, send_ref, scratch_ref, block_ref, sems,
 ):
     del empty_ref
     grain_lane = iota((16, LANE), 1) // 8
-    moved = jnp.where(
-        one_of(grain_lane, (5, 6, 7)),
-        xlo_ref[8:24, :],
-        jnp.where(one_of(grain_lane, (0, 1, 2)), xhi_ref[8:24, :], 0.0),
-    )
+    xlo, xhi = from_rows(place_x_ref, first_ref, other_ref, 8, 16)
+    moved = jnp.where(one_of(grain_lane, (5, 6, 7)), xlo, jnp.where(one_of(grain_lane, (0, 1, 2)), xhi, 0.0))
     moved_parts = jnp.concatenate(split3(moved), axis=0)
     corrections = []
     for bx in range(2):
@@ -305,18 +315,19 @@
     row = iota((8, LANE), 0)
     first_row = jnp.logical_and(row == 0, low_half)
     last_row = jnp.logical_and(row == 7, jnp.logical_not(low_half))
-    turned_low = pltpu.roll(xlo_ref[0:8, :], 64, 1)
-    turned_high = pltpu.roll(xhi_ref[0:8, :], 64, 1)
+    rim_low, rim_high = from_rows(place_x_ref, first_ref, other_ref, 0, 8)
+    turned_low = pltpu.roll(rim_low, 64, 1)
+    turned_high = pltpu.roll(rim_high, 64, 1)
     for q in range(Q):
         for half in range(2):
             part = plane_ref[q, half]
             if CX[q] == 1:
                 k = XUP.index(q)
-                edge = turned_low[k : k + 1] if half else xlo_ref[k : k + 1, :]
+                edge = turned_low[k : k + 1] if half else rim_low[k : k + 1]
                 part = jnp.where(first_row, edge, part)
             elif CX[q] == -1:
                 k = XDN.index(q)
-                edge = xhi_ref[k : k + 1, :] if half else turned_high[k : k + 1]
+                edge = rim_high[k : k + 1] if half else turned_high[k : k + 1]
                 part = jnp.where(last_row, edge, part)
             if q:
                 part = jnp.where(toward_ref[half] == OPP[q], value_ref[q, half] - correction[half], part)
@@ -339,11 +350,6 @@
 
 VMEM = pl.BlockSpec(memory_space=pltpu.VMEM)
 SMEM = pl.BlockSpec(memory_space=pltpu.SMEM)
-
-
-def ring(axis, step):
-    count = lax.axis_size(axis)
-    return [(i, (i + step) % count) for i in range(count)]
 
 
 def near(*arrays):
@@ -371,15 +377,15 @@
     near_pair = lax.all_gather(
         near_msg, "gy", axis=0, tiled=True, axis_index_groups=[[i, i + 1] for i in range(0, columns, 2)]
     )
-    x_up, x_dn = pl.pallas_call(
+    x_first, x_other = pl.pallas_call(
         second_kernel,
         out_shape=(chip(40, LANE), chip(40, LANE)),
-        in_specs=[SMEM] + [VMEM] * 4,
+        in_specs=[SMEM] * 2 + [VMEM] * 4,
         out_specs=(VMEM,) * 2,
         name="x_messages",
-    )(place_y, *near(col, near_msg, near_pair, far_pair))
-    xlo = lax.ppermute(x_up, "gx", ring("gx", 1))
-    xhi = lax.ppermute(x_dn, "gx", ring("gx", -1))
+    )(place_x, place_y, *near(col, near_msg, near_pair, far_pair))
+    first = lax.ppermute(x_first, "gx", [(i, i ^ 1) for i in range(group)])
+    other = lax.ppermute(x_other, "gx", [(i, (i + 2 * (i % 2) - 1) % group) for i in range(group)])
     plane, value, toward, pick, own, arrived, spread, terms = pl.pallas_call(
         prepare_kernel,
         out_shape=(
@@ -397,7 +403,7 @@
         scratch_shapes=[pltpu.VMEM((8, ROWS, LANE), F32)],
         cost_estimate=pl.CostEstimate(flops=4_000_000, bytes_accessed=1_000_000, transcendentals=0),
         name="prepare",
-    )(place_x, place_y, link_lists, *near(col, near_pair, far_pair, x_up), grains, grain_moves, *near(x_dn))
+    )(place_x, place_y, link_lists, *near(col, near_pair, far_pair, x_first), grains, grain_moves, *near(x_other))
     empty = pl.pallas_call(
         clear_kernel,
         out_shape=jax.ShapeDtypeStruct((group * Q, 4, LANE), F32),
@@ -405,27 +411,27 @@
         out_specs=VMEM,
         cost_estimate=pl.CostEstimate(flops=4_000_000, bytes_accessed=1_000_000, transcendentals=0),
         name="clear_slots",
-    )(*near(x_dn))
+    )(*near(x_other))
     send = pl.pallas_call(
         finish_kernel,
         out_shape=jax.ShapeDtypeStruct((group * Q, 4, LANE), F32),
-        in_specs=[SMEM, pl.BlockSpec(memory_space=pl.ANY)] + [VMEM] * 9,
+        in_specs=[SMEM, SMEM, pl.BlockSpec(memory_space=pl.ANY)] + [VMEM] * 9,
         out_specs=pl.BlockSpec(memory_space=pl.ANY),
-        input_output_aliases={1: 0},
+        input_output_aliases={2: 0},
         scratch_shapes=[
             pltpu.VMEM((ROWS, LANE), F32),
             pltpu.VMEM((4, Q, 4, LANE), F32),
             pltpu.SemaphoreType.DMA((4,)),
         ],
         name="finish_blocks",
-    )(owner_map, empty, *near(plane, value, toward, xlo, xhi, pick, arrived, spread, terms))
+    )(owner_map, place_x, empty, *near(plane, value, toward, first, other, pick, arrived, spread, terms))
     table = pl.pallas_call(
         table_kernel,
         out_shape=jax.ShapeDtypeStruct((GV, 1, 320), F32),
-        in_specs=[VMEM] * 4,
+        in_specs=[SMEM] + [VMEM] * 4,
         out_specs=VMEM,
         name="grain_table",
-    )(*near(x_up, xlo, xhi, own))
+    )(place_x, *near(x_first, first, other, own))
     out = lax.all_to_all(send.reshape(group, 1, Q, 512), "gx", split_axis=0, concat_axis=0, tiled=True)
     return (out, table)
 

time: 74 us -> 73.8 us (level)
  waiting for transfers between devices: 34.7 us -> 31.6 us
  starting transfers between devices: 29.4 us -> 32.3 us
    ppermute x2, starting transfers between devices: 15.7 us -> 19.8 us  [the longest x1 15.5 us: body(): first = lax.ppermute(x_first, 'gx', [(i, i ^ 1) for i in range(group)])]
    ppermute x2, waiting for transfers between devices: 3.58 us -> 0.01 us  [the longest x1 0.01 us: body(): lax.ppermute(x_other, 'gx', [(i, (i + 2 * (i % 2) - 1) % group) for i in...]
    all_to_all x1, starting transfers between devices: 6.62 us -> 5.47 us  [body(): lax.all_to_all(send.reshape(group, 1, Q, 512), 'gx', split_axis=0, concat...]
  transfers between devices with their start and end apart: 4 -> 4, of which waited for: 2 -> 1; matrix products, arithmetic and copies ran while one was open for 0% -> 0% of each run, Pallas kernels for 4% -> 4%
where the time goes in v5:
time: 73.8 us; the launch traced here: 73.4 us
  starting transfers between devices  32.3 us (44%)
  waiting for transfers between devices  31.6 us (43%)
  Pallas kernels  6.14 us (8%)
  blocking collectives  1.84 us (2%)
  local copies, waits for them, and re-layouts  0.83 us (1%)
    all_to_all x1, waiting for transfers between devices, body(): lax.all_to_all(send.reshape(group, 1, Q, 512), 'gx', split_axis=0, concat...  31.6 us
    ppermute x1, starting transfers between devices, body(): first = lax.ppermute(x_first, 'gx', [(i, i ^ 1) for i in range(group)])  15.5 us
    ppermute x1, starting transfers between devices, body(): lax.ppermute(far_msg, 'gy', [(i, (i + 2 * (i % 2) - 1) % columns) for i i...  7.01 us
    all_to_all x1, starting transfers between devices, body(): lax.all_to_all(send.reshape(group, 1, Q, 512), 'gx', split_axis=0, concat...  5.47 us
    ppermute x1, starting transfers between devices, body(): lax.ppermute(x_other, 'gx', [(i, (i + 2 * (i % 2) - 1) % group) for i in...  4.28 us
    pallas_call x1, Pallas kernels, body(): pl.pallas_call(finish_kernel, out_shape=jax.ShapeDtypeStruct((group * Q,...  1.86 us
    all_gather x1, blocking collectives, body(): lax.all_gather(near_msg, 'gy', axis=0, tiled=True, axis_index_groups=[[i,...  1.84 us
  transfers between devices with their start and end apart: 4, of which 1 were waited for; matrix products, arithmetic and copies ran while one was open for 0% of the time, Pallas kernels for 4%

profile of v5, /device:TPU:64, one launch (start us, length us, event | category | flops | bytes accessed | tf_op | source)
XLA Modules:
  0.0 73.4 jit_solution(10302427293088329952)
XLA Ops:
  0.6 1.3 %collide_pack.1 = (f32[19,16,128]{2,1,0:T(8,128)S(1)}, f32[48,128]{1,0:T(8,128)S(1)}, f32[48,128]{1,0:T(8,128)S(1)}) custom-call(s32[1]{0:T(128)} %bitcast.1.place_y_ref, f32[19,16,128]{2,1,0:T(8,128)} %pdf_ref.1, f32[26,1,256]{2,1,0:T(1,128)} %grains_ref.3, s32[1,256]{1,0:T(1,128)} %moves_ref.3), custom_call_target="tpu_custom_call" | custom-call | tf_op jit(solution)/shard_map/collide_pack/pallas_call | solution.py:368
  2.0 7.0 %collective-permute-start = (f32[48,128]{1,0:T(8,128)S(1)}, f32[48,128]{1,0:T(8,128)S(1)}, u32[]{:S(2)}, u32[]{:S(2)}) collective-permute-start(f32[48,128]{1,0:T(8,128)S(1)} %get-tuple-element.17), channel_id=1, source_target_pairs={{0,63},{1,2},{2,1},{3,4},{4,3},{5,6},{6,5},{7,8},{8,7},{9,10},{10,... | collective-permute-start | bytes 73736 | tf_op jit(solution)/shard_map/ppermute | solution.py:376
  9.0 1.8 %all_gather.3.near_ref = f32[96,128]{1,0:T(8,128)S(1)} all-gather(f32[48,128]{1,0:T(8,128)S(1)} %get-tuple-element.16.mine_ref), channel_id=1, replica_groups={{0,1},{2,3},{4,5},{6,7},{8,9},{10,11},{12,13},{14,15},{16,17},{18,19},{..., dimensions={0}, use_global_device_ids=true | all-gather | bytes 73728 | tf_op jit(solution)/shard_map/all_gather | solution.py:377
  10.8 0.0 collective-permute-done.far_ref
  10.8 0.1 x_messages.1
  10.9 4.3 %collective-permute-start.2 = (f32[40,128]{1,0:T(8,128)S(1)}, f32[40,128]{1,0:T(8,128)S(1)}, u32[]{:S(2)}, u32[]{:S(2)}) collective-permute-start(f32[40,128]{1,0:T(8,128)S(1)} %get-tuple-element.18.after_ref), channel_id=1, source_target_pairs={{0,960},{64,128},{128,64},{192,256},{256,192},{320,384},{384,320},... | collective-permute-start | bytes 61448 | tf_op jit(solution)/shard_map/ppermute | solution.py:388
  15.2 15.5 %collective-permute-start.1 = (f32[40,128]{1,0:T(8,128)S(1)}, f32[40,128]{1,0:T(8,128)S(1)}, u32[]{:S(2)}, u32[]{:S(2)}) collective-permute-start(f32[40,128]{1,0:T(8,128)S(1)} %get-tuple-element.19.mine_ref), channel_id=1, source_target_pairs={{0,64},{64,0},{128,192},{192,128},{256,320},{320,256},{384,448},{4... | collective-permute-start | bytes 61448 | tf_op jit(solution)/shard_map/ppermute | solution.py:387
  30.7 0.9 %clear_slots.1.empty_ref = f32[304,4,128]{2,1,0:T(4,128)} custom-call(f32[40,128]{1,0:T(8,128)S(1)} %get-tuple-element.18.after_ref), custom_call_target="tpu_custom_call" | custom-call | flops 4000000 | bytes 1000000 | tf_op jit(solution)/shard_map/clear_slots/pallas_call | solution.py:407
  31.6 1.3 %prepare.1 = (f32[19,2,8,128]{3,2,1,0:T(8,128)S(1)}, f32[19,2,8,128]{3,2,1,0:T(8,128)S(1)}, s32[2,8,128]{2,1,0:T(8,128)S(1)}, f32[2,16,512]{2,1,0:T(8,128)S(1)},...) custom-call(s32[1]{0:T(128)} %bitcast.place_x_ref, ...), custom_call_target="tpu_custom_call" | custom-call | flops 4000000 | bytes 1000000 | tf_op jit(solution)/shard_map/prepare/pallas_call | solution.py:389
  32.9 0.0 collective-permute-done.2.other_ref
  33.0 0.0 collective-permute-done.1.first_ref
  33.0 1.9 %finish_blocks.1 = f32[304,4,128]{2,1,0:T(4,128)} custom-call(s32[2,2]{1,0:T(2,128)} %owner_ref.1, s32[1]{0:T(128)} %bitcast.place_x_ref, f32[304,4,128]{2,1,0:T(4,128)} %clear_slots.1.empty_ref, f32[19,2,8,128]{3,2,1,0:T(8,128)S(1)} %get-tuple-element.20.plane_ref, ...), custom_call_target="tpu_custom_call", output_to_operand_aliasing={{}: (2, {})} | custom-call | tf_op jit(solution)/shard_map/finish_blocks/pallas_call | solution.py:415
  34.8 5.5 %all-to-all-start = ((f32[16,1,19,512]{3,1,2,0:T(1,128)}), f32[16,1,19,512]{3,1,2,0:T(1,128)S(1)}, u32[]{:S(2)}, u32[]{:S(2)}) async-start(f32[16,1,19,512]{3,1,2,0:T(1,128)} %bitcast.3), calls=%async_computation | async-start | bytes 1245184 | tf_op jit(solution)/shard_map/all_to_all | solution.py:435
  40.3 0.6 grain_table.1
  40.9 31.6 %all-to-all-done = f32[16,1,19,512]{3,1,2,0:T(1,128)S(1)} async-done(((f32[16,1,19,512]{3,1,2,0:T(1,128)}), f32[16,1,19,512]{3,1,2,0:T(1,128)S(1)}, u32[]{:S(2)}, u32[]{:S(2)}) %all-to-all-start) | async-done | bytes 622624 | tf_op jit(solution)/shard_map/all_to_all | solution.py:435
  72.6 0.8 %copy.13 = f32[16,1,19,512]{3,1,2,0:T(1,128)} copy(f32[16,1,19,512]{3,1,2,0:T(1,128)S(1)} %all-to-all-done) | data formatting | bytes 1245184
Async XLA Ops:
  2.0 8.9 %collective-permute-start = (f32[48,128]{1,0:T(8,128)S(1)}, f32[48,128]{1,0:T(8,128)S(1)}, u32[]{:S(2)}, u32[]{:S(2)}) collective-permute-start(f32[48,128]{1,0:T(8,128)S(1)} %get-tuple-element.17), channel_id=1, source_target_pairs={{0,63},{1,2},{2,1},{3,4},{4,3},{5,6},{6,5},{7,8},{8,7},{9,10},{10,... | collective-permute-start | bytes 73736 | tf_op jit(solution)/shard_map/ppermute | solution.py:376
  10.9 22.0 %collective-permute-start.2 = (f32[40,128]{1,0:T(8,128)S(1)}, f32[40,128]{1,0:T(8,128)S(1)}, u32[]{:S(2)}, u32[]{:S(2)}) collective-permute-start(f32[40,128]{1,0:T(8,128)S(1)} %get-tuple-element.18.after_ref), channel_id=1, source_target_pairs={{0,960},{64,128},{128,64},{192,256},{256,192},{320,384},{384,320},... | collective-permute-start | bytes 61448 | tf_op jit(solution)/shard_map/ppermute | solution.py:388
  15.2 17.7 %collective-permute-start.1 = (f32[40,128]{1,0:T(8,128)S(1)}, f32[40,128]{1,0:T(8,128)S(1)}, u32[]{:S(2)}, u32[]{:S(2)}) collective-permute-start(f32[40,128]{1,0:T(8,128)S(1)} %get-tuple-element.19.mine_ref), channel_id=1, source_target_pairs={{0,64},{64,0},{128,192},{192,128},{256,320},{320,256},{384,448},{4... | collective-permute-start | bytes 61448 | tf_op jit(solution)/shard_map/ppermute | solution.py:387
  34.8 37.8 %all-to-all-start = ((f32[16,1,19,512]{3,1,2,0:T(1,128)}), f32[16,1,19,512]{3,1,2,0:T(1,128)S(1)}, u32[]{:S(2)}, u32[]{:S(2)}) async-start(f32[16,1,19,512]{3,1,2,0:T(1,128)} %bitcast.3), calls=%async_computation | async-start | bytes 1245184 | tf_op jit(solution)/shard_map/all_to_all | solution.py:435

commit v6 on v3

--- a/solution.py
+++ b/solution.py
@@ -162,8 +162,9 @@
     left = place_y_ref[0] % 2 == 0
     low = slice(start, start + size)
     high = slice(48 + start, 48 + start + size)
-    ylo = jnp.where(left, far_ref[low, :], near_ref[low, :])
-    yhi = jnp.where(left, near_ref[high, :], far_ref[high, :])
+    far = far_ref[low, :]
+    ylo = jnp.where(left, far, near_ref[low, :])
+    yhi = jnp.where(left, near_ref[high, :], far)
     return ylo, yhi
 
 
@@ -333,12 +334,6 @@
     return [(i, (i + step) % count) for i in range(count)]
 
 
-def pair_gather(message, axis, first):
-    count = lax.axis_size(axis)
-    groups = [[i, (i + 1) % count] for i in range(first, count, 2)]
-    return lax.all_gather(message, axis, axis=0, tiled=True, axis_index_groups=groups)
-
-
 def near(*arrays):
     return tuple(pltpu.with_memory_space_constraint(a, pltpu.VMEM) for a in arrays)
 
@@ -359,9 +354,11 @@
         out_specs=(VMEM,) * 3,
         name="collide_pack",
     )(place_y, pdf, grains, grain_moves)
-    near_pair = pair_gather(near_msg, "gy", 0)
-    near_pair, far_msg = lax.optimization_barrier((near_pair, far_msg))
-    far_pair = pair_gather(far_msg, "gy", 1)
+    columns = lax.axis_size("gy")
+    far_pair = lax.ppermute(far_msg, "gy", [(i, (i + 2 * (i % 2) - 1) % columns) for i in range(columns)])
+    near_pair = lax.all_gather(
+        near_msg, "gy", axis=0, tiled=True, axis_index_groups=[[i, i + 1] for i in range(0, columns, 2)]
+    )
     x_up, x_dn = pl.pallas_call(
         second_kernel,
         out_shape=(chip(40, LANE), chip(40, LANE)),

time: 74.1 us -> 74.3 us (level)
  the two profiles are of different devices: /device:TPU:31 before, /device:TPU:63 now
where the time goes in v6:
time: 74.3 us; the launch traced here: 73.9 us
  waiting for transfers between devices  35 us (47%)
  starting transfers between devices  30.1 us (41%)
  Pallas kernels  5.39 us (7%)
  blocking collectives  1.84 us (2%)
  local copies, waits for them, and re-layouts  0.83 us (1%)
    all_to_all x1, waiting for transfers between devices, body(): lax.all_to_all(send.reshape(group, 1, Q, 512), 'gx', split_axis=0, concat...  32.6 us
    ppermute x1, starting transfers between devices, body(): lax.ppermute(far_msg, 'gy', [(i, (i + 2 * (i % 2) - 1) % columns) for i i...  14.5 us
    ppermute x1, starting transfers between devices, body(): xhi = lax.ppermute(x_dn, 'gx', ring('gx', -1))  10 us
    all_to_all x1, starting transfers between devices, body(): lax.all_to_all(send.reshape(group, 1, Q, 512), 'gx', split_axis=0, concat...  3.59 us
    ppermute x1, waiting for transfers between devices, body(): xlo = lax.ppermute(x_up, 'gx', ring('gx', 1))  2.49 us
    pallas_call x1, Pallas kernels, body(): pl.pallas_call(finish_kernel, out_shape=jax.ShapeDtypeStruct((group * Q,...  2.01 us
    ppermute x1, starting transfers between devices, body(): xlo = lax.ppermute(x_up, 'gx', ring('gx', 1))  1.92 us
    all_gather x1, blocking collectives, body(): lax.all_gather(near_msg, 'gy', axis=0, tiled=True, axis_index_groups=[[i,...  1.84 us
  transfers between devices with their start and end apart: 4, of which 2 were waited for; matrix products, arithmetic and copies ran while one was open for 0% of the time, Pallas kernels for 3%

profile of v6, /device:TPU:63, one launch (start us, length us, event | category | flops | bytes accessed | tf_op | source)
XLA Modules:
  0.0 73.9 jit_solution(17867139065460075690)
XLA Ops:
  0.6 1.3 %collide_pack.1 = (f32[19,16,128]{2,1,0:T(8,128)S(1)}, f32[48,128]{1,0:T(8,128)S(1)}, f32[48,128]{1,0:T(8,128)S(1)}) custom-call(s32[1]{0:T(128)} %bitcast.1.place_y_ref, f32[19,16,128]{2,1,0:T(8,128)} %pdf_ref.1, f32[26,1,256]{2,1,0:T(1,128)} %grains_ref.3, s32[1,256]{1,0:T(1,128)} %moves_ref.3), custom_call_target="tpu_custom_call" | custom-call | tf_op jit(solution)/shard_map/collide_pack/pallas_call | solution.py:350
  2.0 14.5 %collective-permute-start = (f32[48,128]{1,0:T(8,128)S(1)}, f32[48,128]{1,0:T(8,128)S(1)}, u32[]{:S(2)}, u32[]{:S(2)}) collective-permute-start(f32[48,128]{1,0:T(8,128)S(1)} %get-tuple-element.17), channel_id=1, source_target_pairs={{0,63},{1,2},{2,1},{3,4},{4,3},{5,6},{6,5},{7,8},{8,7},{9,10},{10,... | collective-permute-start | bytes 73736 | tf_op jit(solution)/shard_map/ppermute | solution.py:358
  16.5 1.8 %all_gather.3.near_ref = f32[96,128]{1,0:T(8,128)S(1)} all-gather(f32[48,128]{1,0:T(8,128)S(1)} %get-tuple-element.16.mine_ref), channel_id=1, replica_groups={{0,1},{2,3},{4,5},{6,7},{8,9},{10,11},{12,13},{14,15},{16,17},{18,19},{..., dimensions={0}, use_global_device_ids=true | all-gather | bytes 73728 | tf_op jit(solution)/shard_map/all_gather | solution.py:359
  18.3 0.0 collective-permute-done.far_ref
  18.3 0.1 x_messages.1
  18.4 10.0 %collective-permute-start.2 = (f32[40,128]{1,0:T(8,128)S(1)}, f32[40,128]{1,0:T(8,128)S(1)}, u32[]{:S(2)}, u32[]{:S(2)}) collective-permute-start(f32[40,128]{1,0:T(8,128)S(1)} %get-tuple-element.19.after_ref), channel_id=1, source_target_pairs={{0,960},{64,0},{128,64},{192,128},{256,192},{320,256},{384,320},{4... | collective-permute-start | bytes 61448 | tf_op jit(solution)/shard_map/ppermute | solution.py:370
  28.5 1.9 %collective-permute-start.1 = (f32[40,128]{1,0:T(8,128)S(1)}, f32[40,128]{1,0:T(8,128)S(1)}, u32[]{:S(2)}, u32[]{:S(2)}) collective-permute-start(f32[40,128]{1,0:T(8,128)S(1)} %get-tuple-element.18.mine_ref), channel_id=1, source_target_pairs={{0,64},{64,128},{128,192},{192,256},{256,320},{320,384},{384,448},... | collective-permute-start | bytes 61448 | tf_op jit(solution)/shard_map/ppermute | solution.py:369
  30.4 1.3 %prepare.1 = (f32[19,2,8,128]{3,2,1,0:T(8,128)S(1)}, f32[19,2,8,128]{3,2,1,0:T(8,128)S(1)}, s32[2,8,128]{2,1,0:T(8,128)S(1)}, f32[2,16,512]{2,1,0:T(8,128)S(1)},...) custom-call(s32[1]{0:T(128)} %bitcast.place_x_ref, ...), custom_call_target="tpu_custom_call" | custom-call | flops 4000000 | bytes 1000000 | tf_op jit(solution)/shard_map/prepare/pallas_call | solution.py:371
  31.7 0.0 collective-permute-done.2.xhi_ref
  31.7 2.5 %collective-permute-done.1.xlo_ref = f32[40,128]{1,0:T(8,128)S(1)} collective-permute-done((f32[40,128]{1,0:T(8,128)S(1)}, f32[40,128]{1,0:T(8,128)S(1)}, u32[]{:S(2)}, u32[]{:S(2)}) %collective-permute-start.1) | collective-permute-done | bytes 20512 | tf_op jit(solution)/shard_map/ppermute | solution.py:369
  34.2 2.0 %finish_blocks.1 = f32[304,4,128]{2,1,0:T(4,128)} custom-call(s32[2,2]{1,0:T(2,128)} %owner_ref.1, f32[19,2,8,128]{3,2,1,0:T(8,128)S(1)} %get-tuple-element.20.plane_ref, f32[19,2,8,128]{3,2,1,0:T(8,128)S(1)} %get-tuple-element.21.value_ref, s32[2,8,128]{2,1,0:T(8,128)S(1)} %get-tuple-element.22.toward_ref, f32[40,128]{1,0:T(8,128)S(1)} %collective-permute-done.1.xlo_ref, ...), custom_call_target="tpu_custom_call" | custom-call | tf_op jit(solution)/shard_map/finish_blocks/pallas_call | solution.py:389
  36.2 3.6 %all-to-all-start = ((f32[16,1,19,512]{3,1,2,0:T(1,128)}), f32[16,1,19,512]{3,1,2,0:T(1,128)S(1)}, u32[]{:S(2)}, u32[]{:S(2)}) async-start(f32[16,1,19,512]{3,1,2,0:T(1,128)} %bitcast.3), calls=%async_computation | async-start | bytes 1245184 | tf_op jit(solution)/shard_map/all_to_all | solution.py:404
  39.8 0.6 grain_table.1
  40.5 32.6 %all-to-all-done = f32[16,1,19,512]{3,1,2,0:T(1,128)S(1)} async-done(((f32[16,1,19,512]{3,1,2,0:T(1,128)}), f32[16,1,19,512]{3,1,2,0:T(1,128)S(1)}, u32[]{:S(2)}, u32[]{:S(2)}) %all-to-all-start) | async-done | bytes 622624 | tf_op jit(solution)/shard_map/all_to_all | solution.py:404
  73.0 0.8 %copy.11 = f32[16,1,19,512]{3,1,2,0:T(1,128)} copy(f32[16,1,19,512]{3,1,2,0:T(1,128)S(1)} %all-to-all-done) | data formatting | bytes 1245184
Async XLA Ops:
  2.0 16.4 %collective-permute-start = (f32[48,128]{1,0:T(8,128)S(1)}, f32[48,128]{1,0:T(8,128)S(1)}, u32[]{:S(2)}, u32[]{:S(2)}) collective-permute-start(f32[48,128]{1,0:T(8,128)S(1)} %get-tuple-element.17), channel_id=1, source_target_pairs={{0,63},{1,2},{2,1},{3,4},{4,3},{5,6},{6,5},{7,8},{8,7},{9,10},{10,... | collective-permute-start | bytes 73736 | tf_op jit(solution)/shard_map/ppermute | solution.py:358
  18.4 13.3 %collective-permute-start.2 = (f32[40,128]{1,0:T(8,128)S(1)}, f32[40,128]{1,0:T(8,128)S(1)}, u32[]{:S(2)}, u32[]{:S(2)}) collective-permute-start(f32[40,128]{1,0:T(8,128)S(1)} %get-tuple-element.19.after_ref), channel_id=1, source_target_pairs={{0,960},{64,0},{128,64},{192,128},{256,192},{320,256},{384,320},{4... | collective-permute-start | bytes 61448 | tf_op jit(solution)/shard_map/ppermute | solution.py:370
  28.5 5.7 %collective-permute-start.1 = (f32[40,128]{1,0:T(8,128)S(1)}, f32[40,128]{1,0:T(8,128)S(1)}, u32[]{:S(2)}, u32[]{:S(2)}) collective-permute-start(f32[40,128]{1,0:T(8,128)S(1)} %get-tuple-element.18.mine_ref), channel_id=1, source_target_pairs={{0,64},{64,128},{128,192},{192,256},{256,320},{320,384},{384,448},... | collective-permute-start | bytes 61448 | tf_op jit(solution)/shard_map/ppermute | solution.py:369
  36.2 36.8 %all-to-all-start = ((f32[16,1,19,512]{3,1,2,0:T(1,128)}), f32[16,1,19,512]{3,1,2,0:T(1,128)S(1)}, u32[]{:S(2)}, u32[]{:S(2)}) async-start(f32[16,1,19,512]{3,1,2,0:T(1,128)} %bitcast.3), calls=%async_computation | async-start | bytes 1245184 | tf_op jit(solution)/shard_map/all_to_all | solution.py:404
